TPU v7x, 256 devices: a whole 4x4x8 slice. The times are simulated.
256 devices in a mesh: depth: 16 (over x, z_lo), plane: 16 (over z_hi, y, core).
Axes of the slice: x: 4, y: 4, z: 8 (z_hi: 2, z_lo: 4; z = z_hi * 4 + z_lo), core: 2. Of those that a mesh axis runs over, the one named last changes fastest.
Arguments:
- spectrum: bfloat16 [32, 2, 1024, 2048], P('depth', None, 'plane'), may hold values from -6 to 6
- colour_table: float32 [4, 4, 16], replicated, may hold values from 0 to 1
- map_index: int32 [32], P('depth'), may hold values from 0 to 3
Outputs:
- final_image: float32 [4, 2048, 2048], P(None, 'plane', 'depth')
Inputs may be any that keep to these rules, and one draw needn't show every extreme that they name: `map_index`: which of the 4 colour maps each depth plane uses.
All inputs are finite; a program needn't handle non-finite values.
Results may differ from a plain program's by a relative error of at most 0.0034.
Values may be sent and summed in bfloat16 or wider, within the bound.
A program may use at most 64 MiB of HBM per device.

v0:
```python
import functools
import math

import jax
import jax.numpy as jnp
import numpy as np
from jax import lax
from jax.experimental import pallas as pl
from jax.experimental.pallas import tpu as pltpu
from jax.sharding import PartitionSpec as P

NX = 2048
NY = 2048
NCTRL = 16
NMAPS = 4
SPREAD = 3.0
OPACITY = 0.06
LANES = 128
FINE = 16
CHUNKS = 2
MESH = pl.DeviceIdType.MESH


def base_tables():
    fine = 2.0 * np.pi * np.outer(np.arange(FINE), np.arange(NX)) / NX
    coarse = 2.0 * np.pi * (np.outer(np.arange(128), np.arange(128)) % 128) / 128.0
    fine_pair = np.stack([np.cos(fine), np.sin(fine)]).astype(np.float32)
    coarse_pair = np.stack([np.cos(coarse), np.sin(coarse)]).astype(np.float32)
    return fine_pair, coarse_pair


def kernel(
    spec_ref, colour_ref, map_ref, fine_ref, coarse_ref, out_ref,
    swap_ref, cos_ref, sin_ref, send1, recv1, ytab, lhs, ctab, dens, send2, recv2,
    send_sem, recv1_sem, recv2_sem, tab_sem, *, comm
):
    if comm:
        depth_id = lax.axis_index("depth")
        plane_id = lax.axis_index("plane")
    else:
        depth_id = jnp.int32(5)
        plane_id = jnp.int32(6)
    my_x, my_zl = depth_id // 4, depth_id % 4
    my_zh, my_j = plane_id // 8, plane_id % 8
    my_z = my_zh * 4 + my_zl

    def same_x(z, j):
        return {"depth": my_x * 4 + z % 4, "plane": (z // 4) * 8 + j}

    def same_plane(x, zl):
        return {"depth": x * 4 + zl, "plane": plane_id}

    if comm:
        barrier = pltpu.get_barrier_semaphore()

        def greet_gather(i, carry):
            z, j = (my_z + i // 8) % 8, (my_j + i % 8) % 8
            pl.semaphore_signal(barrier, inc=1, device_id=same_x(z, j), device_id_type=MESH)
            return carry

        def greet_depth(i, carry):
            x, zl = (my_x + 1 + i // 4) % 4, i % 4
            pl.semaphore_signal(barrier, inc=1, device_id=same_plane(x, zl), device_id_type=MESH)
            return carry

        lax.fori_loop(1, 64, greet_gather, 0)
        lax.fori_loop(0, 12, greet_depth, 0)

    for z in range(2):
        swap_ref[z * 128 : z * 128 + 64, :] = -spec_ref[z, 1]
        swap_ref[z * 128 + 64 : z * 128 + 128, :] = spec_ref[z, 0]

    for z in range(2):
        values = colour_ref[map_ref[z]]
        values = jnp.concatenate([values, jnp.zeros((4, LANES - NCTRL), jnp.float32)], axis=1)
        row = lax.broadcasted_iota(jnp.int32, (4, LANES), 0)
        values = jnp.where(row == 3, values * OPACITY, values)
        slopes = pltpu.roll(values, LANES - 1, 1) - values
        ctab[my_zl, z] = jnp.concatenate([values, slopes], axis=0)

    if comm:
        pl.semaphore_wait(barrier, 75)
        for k in range(1, 4):
            pltpu.make_async_remote_copy(
                src_ref=ctab.at[my_zl], dst_ref=ctab.at[my_zl], send_sem=send_sem.at[2 * CHUNKS],
                recv_sem=tab_sem, device_id=same_plane(my_x, (my_zl + k) % 4), device_id_type=MESH,
            ).start()

    x_scale = 1.0 / math.sqrt(NX)
    y_scale = math.sqrt(2.0 / NY)

    def coarse_row(index, scale):
        bc = coarse_ref[0, pl.ds(index, 1), :] * scale
        bs = coarse_ref[1, pl.ds(index, 1), :] * scale
        return jnp.broadcast_to(bc, (FINE, LANES)), jnp.broadcast_to(bs, (FINE, LANES))

    def transform_x(step, carry):
        chunk, k = step // 8, step % 8
        z = (my_z + 4 + ((k + 1) // 2) * (1 - 2 * (k % 2))) % 8
        first = (z // 4) * 64 + 2 * (z % 4) + chunk
        for j in range(8):
            bc, bs = coarse_row(first + 8 * j, x_scale)
            for b in range(NX // LANES):
                cols = slice(b * LANES, (b + 1) * LANES)
                ec, es = fine_ref[0, :, cols], fine_ref[1, :, cols]
                cos_ref[j * FINE : (j + 1) * FINE, cols] = (bc * ec - bs * es).astype(jnp.bfloat16)
                sin_ref[j * FINE : (j + 1) * FINE, cols] = (bs * ec + bc * es).astype(jnp.bfloat16)
        nt = (((1,), (1,)), ((), ()))
        spec = spec_ref[...].reshape(256, NX)
        rows = lax.dot_general(cos_ref[...], spec, nt, preferred_element_type=jnp.float32)
        rows += lax.dot_general(sin_ref[...], swap_ref[...], nt, preferred_element_type=jnp.float32)
        rows = rows.astype(jnp.bfloat16).reshape(8, FINE, 256)
        send1[chunk, k] = rows
        if comm:
            def send(i, c):
                j = (my_j + i) % 8

                @pl.when(jnp.logical_or(k != 7, i != 0))
                def _():
                    pltpu.make_async_remote_copy(
                        src_ref=send1.at[chunk, k, j], dst_ref=recv1.at[chunk, my_zl * 16 + plane_id],
                        send_sem=send_sem.at[chunk], recv_sem=recv1_sem.at[chunk],
                        device_id=same_x(z, j), device_id_type=MESH,
                    ).start()

                return c

            lax.fori_loop(0, 8, send, 0)

        @pl.when(k == 7)
        def _():
            recv1[chunk, my_zl * 16 + plane_id] = send1[chunk, k, my_j]

        return carry

    lax.fori_loop(0, 8 * CHUNKS, transform_x, 0)

    def make_y(a, carry):
        bc, bs = coarse_row(a, y_scale)
        base = pl.multiple_of((a // 4) * 128 + (a % 4) * FINE, FINE)
        for b in range(NY // LANES):
            cols = slice(b * LANES, (b + 1) * LANES)
            ec, es = fine_ref[0, :, cols], fine_ref[1, :, cols]
            part = slice((b % 2) * LANES, (b % 2 + 1) * LANES)
            ytab[b // 2, pl.ds(base, FINE), part] = (bc * ec - bs * es).astype(jnp.bfloat16)
            ytab[b // 2, pl.ds(base + 64, FINE), part] = (-(bs * ec + bc * es)).astype(jnp.bfloat16)
        return carry

    lax.fori_loop(0, 64, make_y, 0)

    if comm:
        pltpu.make_async_remote_copy(
            src_ref=ctab.at[pl.ds(0, 3)], dst_ref=ctab.at[pl.ds(0, 3)], send_sem=send_sem.at[2 * CHUNKS],
            recv_sem=tab_sem, device_id=same_plane(my_x, (my_zl + 1) % 4), device_id_type=MESH,
        ).wait_recv()

    for chunk in range(CHUNKS):
        if comm:
            pltpu.make_async_remote_copy(
                src_ref=recv1.at[chunk, pl.ds(0, 63)], dst_ref=recv1.at[chunk, pl.ds(0, 63)],
                send_sem=send_sem.at[chunk], recv_sem=recv1_sem.at[chunk],
                device_id=same_x((my_z + 1) % 8, my_j), device_id_type=MESH,
            ).wait_recv()
        for zl in range(4):
            for z in range(2):
                for p in range(16):
                    lhs[(2 * zl + z) * FINE : (2 * zl + z + 1) * FINE, p * LANES : (p + 1) * LANES] = (
                        recv1[chunk, zl * 16 + p, :, z * LANES : (z + 1) * LANES]
                    )

        def columns(step, carry, chunk=chunk):
            block = (depth_id // 2 + 1 + step) % 8
            dens[...] = jnp.dot(lhs[...], ytab[block], preferred_element_type=jnp.float32)
            tiles = [(r, c) for c in range(2) for r in range(2)]
            colour = {t: [jnp.zeros((8, LANES), jnp.float32) for _ in range(3)] for t in tiles}
            clear = {t: jnp.ones((8, LANES), jnp.float32) for t in tiles}
            for z in range(8):
                maps = [
                    jnp.broadcast_to(ctab[z // 2, z % 2, q : q + 1, :], (8, LANES)) for q in range(8)
                ]
                for r, c in tiles:
                    d = dens[z * FINE + 8 * r : z * FINE + 8 * r + 8, c * LANES : (c + 1) * LANES]
                    position = jnp.clip((d + SPREAD) * ((NCTRL - 1) / (2.0 * SPREAD)), 0.0, NCTRL - 1.0)
                    index = position.astype(jnp.int32)
                    frac = position - index.astype(jnp.float32)
                    value = [
                        jnp.take_along_axis(maps[q], index, axis=1, mode="promise_in_bounds")
                        + frac * jnp.take_along_axis(maps[q + 4], index, axis=1, mode="promise_in_bounds")
                        for q in range(4)
                    ]
                    weight = clear[r, c] * value[3]
                    colour[r, c] = [colour[r, c][q] + weight * value[q] for q in range(3)]
                    clear[r, c] = clear[r, c] - weight
            for c in range(2):
                d = block * 2 + c
                for q in range(4):
                    both = jnp.concatenate(
                        [colour[r, c][q] if q < 3 else 1.0 - clear[r, c] for r in range(2)], axis=0
                    )
                    send2[chunk, d, q] = both.astype(jnp.bfloat16)
                x, zl = d // 4, d % 4
                if comm:
                    @pl.when(d != depth_id)
                    def _():
                        pltpu.make_async_remote_copy(
                            src_ref=send2.at[chunk, d], dst_ref=recv2.at[chunk, depth_id],
                            send_sem=send_sem.at[CHUNKS + chunk], recv_sem=recv2_sem.at[chunk],
                            device_id=same_plane(x, zl), device_id_type=MESH,
                        ).start()
            return carry

        lax.fori_loop(0, 8, columns, 0)
        recv2[chunk, depth_id] = send2[chunk, depth_id]

    for chunk in range(CHUNKS):
        if comm:
            pltpu.make_async_remote_copy(
                src_ref=recv2.at[chunk, pl.ds(0, 15)], dst_ref=recv2.at[chunk, pl.ds(0, 15)],
                send_sem=send_sem.at[CHUNKS + chunk], recv_sem=recv2_sem.at[chunk],
                device_id=same_plane((my_x + 1) % 4, my_zl), device_id_type=MESH,
            ).wait_recv()
        for zl in range(4):
            rows = slice(zl * 32 + chunk * FINE, zl * 32 + (chunk + 1) * FINE)
            total = [recv2[chunk, zl, q].astype(jnp.float32) for q in range(3)]
            clear = 1.0 - recv2[chunk, zl, 3].astype(jnp.float32)
            for x in range(1, 4):
                for q in range(3):
                    total[q] = total[q] + clear * recv2[chunk, 4 * x + zl, q].astype(jnp.float32)
                clear = clear * (1.0 - recv2[chunk, 4 * x + zl, 3].astype(jnp.float32))
            for q in range(3):
                out_ref[q, rows, :] = total[q]
            out_ref[3, rows, :] = clear

    if comm:
        for chunk in range(CHUNKS):
            pltpu.make_async_remote_copy(
                src_ref=recv1.at[chunk, pl.ds(0, 63)], dst_ref=recv1.at[chunk, pl.ds(0, 63)],
                send_sem=send_sem.at[chunk], recv_sem=recv1_sem.at[chunk],
                device_id=same_x((my_z + 1) % 8, my_j), device_id_type=MESH,
            ).wait_send()
            pltpu.make_async_remote_copy(
                src_ref=recv2.at[chunk, pl.ds(0, 15)], dst_ref=recv2.at[chunk, pl.ds(0, 15)],
                send_sem=send_sem.at[CHUNKS + chunk], recv_sem=recv2_sem.at[chunk],
                device_id=same_plane((my_x + 1) % 4, my_zl), device_id_type=MESH,
            ).wait_send()
        pltpu.make_async_remote_copy(
            src_ref=ctab.at[pl.ds(0, 3)], dst_ref=ctab.at[pl.ds(0, 3)], send_sem=send_sem.at[2 * CHUNKS],
            recv_sem=tab_sem, device_id=same_plane(my_x, (my_zl + 1) % 4), device_id_type=MESH,
        ).wait_send()


def render(spectrum, colour_table, map_index, comm=True):
    fine_pair, coarse_pair = base_tables()
    vmem = pl.BlockSpec(memory_space=pltpu.VMEM)
    bf16, f32 = jnp.bfloat16, jnp.float32
    return pl.pallas_call(
        functools.partial(kernel, comm=comm),
        out_shape=jax.ShapeDtypeStruct((4, 128, 128), f32),
        in_specs=[vmem, vmem, pl.BlockSpec(memory_space=pltpu.SMEM), vmem, vmem],
        out_specs=vmem,
        scratch_shapes=[
            pltpu.VMEM((256, NX), bf16),
            pltpu.VMEM((128, NX), bf16),
            pltpu.VMEM((128, NX), bf16),
            pltpu.VMEM((CHUNKS, 8, 8, FINE, 256), bf16),
            pltpu.VMEM((CHUNKS, 64, FINE, 256), bf16),
            pltpu.VMEM((8, NY, 256), bf16),
            pltpu.VMEM((128, NY), bf16),
            pltpu.VMEM((4, 2, 8, LANES), f32),
            pltpu.VMEM((128, 256), f32),
            pltpu.VMEM((CHUNKS, 16, 4, FINE, LANES), bf16),
            pltpu.VMEM((CHUNKS, 16, 4, FINE, LANES), bf16),
            pltpu.SemaphoreType.DMA((2 * CHUNKS + 1,)),
            pltpu.SemaphoreType.DMA((CHUNKS,)),
            pltpu.SemaphoreType.DMA((CHUNKS,)),
            pltpu.SemaphoreType.DMA,
        ],
        compiler_params=pltpu.CompilerParams(
            vmem_limit_bytes=40 << 20,
            **(dict(collective_id=0, has_side_effects=True) if comm else {}),
        ),
        name="render",
    )(spectrum, colour_table, map_index, jnp.asarray(fine_pair), jnp.asarray(coarse_pair))


def solution(mesh):
    return jax.shard_map(
        render,
        mesh=mesh,
        in_specs=(P("depth", None, "plane", None), P(), P("depth")),
        out_specs=P(None, "plane", "depth"),
        check_vma=False,
    )
```

profile of v0, /device:TPU:1, one launch (start us, length us, event | category | flops | bytes accessed | tf_op | source)
XLA Modules:
  0.0 56.1 jit_solution(12202210638316719854)
XLA Ops:
  0.0 0.0 copy-start
  0.0 1.2 %copy-done = bf16[2,2,64,2048]{3,2,1,0:T(8,128)(2,1)S(1)} copy-done((bf16[2,2,64,2048]{3,2,1,0:T(8,128)(2,1)S(1)}, bf16[2,2,64,2048]{3,2,1,0:T(8,128)(2,1)}, u32[]{:S(2)}) %copy-start) | copy-done | bytes 1048600
  1.2 0.0 copy-start.1
  1.2 0.9 %copy-done.1 = f32[2,16,2048]{2,1,0:T(8,128)S(1)} copy-done((f32[2,16,2048]{2,1,0:T(8,128)S(1)}, f32[2,16,2048]{2,1,0:T(8,128)}, u32[]{:S(2)}) %copy-start.1) | copy-done | bytes 262168
  2.2 0.0 copy-start.2
  2.2 0.9 %copy-done.2 = f32[2,128,128]{2,1,0:T(8,128)S(1)} copy-done((f32[2,128,128]{2,1,0:T(8,128)S(1)}, f32[2,128,128]{2,1,0:T(8,128)}, u32[]{:S(2)}) %copy-start.2) | copy-done | bytes 131096
  3.1 0.0 copy-start.3
  3.1 0.7 %copy-done.3 = f32[4,4,16]{2,1,0:T(4,128)S(1)} copy-done((f32[4,4,16]{2,1,0:T(4,128)S(1)}, f32[4,4,16]{2,1,0:T(4,128)}, u32[]{:S(2)}) %copy-start.3) | copy-done | bytes 1048
  3.8 0.0 copy-start.4
  3.8 0.7 %copy-done.4 = s32[2]{0:T(128)S(1)} copy-done((s32[2]{0:T(128)S(1)}, s32[2]{0:T(128)}, u32[]{:S(2)}) %copy-start.4) | copy-done | bytes 32
  4.4 50.9 %render.1 = f32[4,128,128]{2,1,0:T(8,128)S(1)} custom-call(bf16[2,2,64,2048]{3,2,1,0:T(8,128)(2,1)S(1)} %copy-done, f32[4,4,16]{2,1,0:T(4,128)S(1)} %copy-done.3, s32[2]{0:T(128)S(1)} %copy-done.4, f32[2,16,2048]{2,1,0:T(8,128)S(1)} %copy-done.1, f32[2,128,128]{2,1,0:T(8,128)S(1)} %copy-done.2), custom_call_target="tpu_custom_call" | custom-call | tf_op jit(solution)/shard_map/render/pallas_call | solution.py:256
  55.4 0.7 %copy.7 = f32[4,128,128]{2,1,0:T(8,128)} copy(f32[4,128,128]{2,1,0:T(8,128)S(1)} %render.1) | data formatting | bytes 524288
Async XLA Ops:
  0.0 1.2 %copy-start = (bf16[2,2,64,2048]{3,2,1,0:T(8,128)(2,1)S(1)}, bf16[2,2,64,2048]{3,2,1,0:T(8,128)(2,1)}, u32[]{:S(2)}) copy-start(bf16[2,2,64,2048]{3,2,1,0:T(8,128)(2,1)} %spec_ref.1) | copy-start | bytes 3145732
  1.2 0.9 %copy-start.1 = (f32[2,16,2048]{2,1,0:T(8,128)S(1)}, f32[2,16,2048]{2,1,0:T(8,128)}, u32[]{:S(2)}) copy-start(f32[2,16,2048]{2,1,0:T(8,128)} %constant.4.clone.fine_ref) | copy-start | bytes 786436
  2.2 0.9 %copy-start.2 = (f32[2,128,128]{2,1,0:T(8,128)S(1)}, f32[2,128,128]{2,1,0:T(8,128)}, u32[]{:S(2)}) copy-start(f32[2,128,128]{2,1,0:T(8,128)} %constant.5.clone.coarse_ref) | copy-start | bytes 393220
  3.1 0.7 %copy-start.3 = (f32[4,4,16]{2,1,0:T(4,128)S(1)}, f32[4,4,16]{2,1,0:T(4,128)}, u32[]{:S(2)}) copy-start(f32[4,4,16]{2,1,0:T(4,128)} %colour_ref.1) | copy-start | bytes 3076
  3.8 0.7 %copy-start.4 = (s32[2]{0:T(128)S(1)}, s32[2]{0:T(128)}, u32[]{:S(2)}) copy-start(s32[2]{0:T(128)} %map_ref.1) | copy-start | bytes 28
where the time goes:
time: 56.3 us; the launch traced here: 56.1 us
  Pallas kernels  50.9 us (90%)
  local copies, waits for them, and re-layouts  5.13 us (9%)
    pallas_call x1, Pallas kernels, render(): pl.pallas_call(functools.partial(kernel, comm=comm), out_shape=jax.ShapeD...  50.9 us
    unnamed x11, local copies, waits for them, and re-layouts  5.13 us

commit v1 on v0

--- a/solution.py
+++ b/solution.py
@@ -30,9 +30,10 @@
 
 
 def kernel(
-    spec_ref, colour_ref, map_ref, fine_ref, coarse_ref, out_ref,
-    swap_ref, cos_ref, sin_ref, send1, recv1, ytab, lhs, ctab, dens, send2, recv2,
-    send_sem, recv1_sem, recv2_sem, tab_sem, *, comm
+    spec_hbm, colour_hbm, map_hbm, fine_hbm, coarse_hbm, out_ref,
+    spec_ref, colour_ref, map_ref, fine_ref, coarse_ref,
+    swap_ref, cos_ref, sin_ref, send1, recv1, ytab, lhs, ctab, dens, send2, recv2, send3,
+    in_sem, send_sem, recv1_sem, recv2_sem, recv3_sem, tab_sem, *, comm
 ):
     if comm:
         depth_id = lax.axis_index("depth")
@@ -44,6 +45,16 @@
     my_zh, my_j = plane_id // 8, plane_id % 8
     my_z = my_zh * 4 + my_zl
 
+    fetches = [
+        pltpu.make_async_copy(src, dst, in_sem.at[i])
+        for i, (src, dst) in enumerate(
+            [(spec_hbm, spec_ref), (fine_hbm, fine_ref), (coarse_hbm, coarse_ref),
+             (colour_hbm, colour_ref), (map_hbm, map_ref)]
+        )
+    ]
+    for fetch in fetches:
+        fetch.start()
+
     def same_x(z, j):
         return {"depth": my_x * 4 + z % 4, "plane": (z // 4) * 8 + j}
 
@@ -59,12 +70,16 @@
             return carry
 
         def greet_depth(i, carry):
-            x, zl = (my_x + 1 + i // 4) % 4, i % 4
-            pl.semaphore_signal(barrier, inc=1, device_id=same_plane(x, zl), device_id_type=MESH)
+            pl.semaphore_signal(
+                barrier, inc=1, device_id=same_plane((my_x + i) % 4, my_zl), device_id_type=MESH
+            )
             return carry
 
         lax.fori_loop(1, 64, greet_gather, 0)
-        lax.fori_loop(0, 12, greet_depth, 0)
+        lax.fori_loop(1, 4, greet_depth, 0)
+
+    for fetch in fetches:
+        fetch.wait()
 
     for z in range(2):
         swap_ref[z * 128 : z * 128 + 64, :] = -spec_ref[z, 1]
@@ -79,10 +94,10 @@
         ctab[my_zl, z] = jnp.concatenate([values, slopes], axis=0)
 
     if comm:
-        pl.semaphore_wait(barrier, 75)
+        pl.semaphore_wait(barrier, 66)
         for k in range(1, 4):
             pltpu.make_async_remote_copy(
-                src_ref=ctab.at[my_zl], dst_ref=ctab.at[my_zl], send_sem=send_sem.at[2 * CHUNKS],
+                src_ref=ctab.at[my_zl], dst_ref=ctab.at[my_zl], send_sem=send_sem.at[3 * CHUNKS],
                 recv_sem=tab_sem, device_id=same_plane(my_x, (my_zl + k) % 4), device_id_type=MESH,
             ).start()
 
@@ -150,7 +165,7 @@
 
     if comm:
         pltpu.make_async_remote_copy(
-            src_ref=ctab.at[pl.ds(0, 3)], dst_ref=ctab.at[pl.ds(0, 3)], send_sem=send_sem.at[2 * CHUNKS],
+            src_ref=ctab.at[pl.ds(0, 3)], dst_ref=ctab.at[pl.ds(0, 3)], send_sem=send_sem.at[3 * CHUNKS],
             recv_sem=tab_sem, device_id=same_plane(my_x, (my_zl + 1) % 4), device_id_type=MESH,
         ).wait_recv()
 
@@ -169,7 +184,9 @@
                     )
 
         def columns(step, carry, chunk=chunk):
-            block = (depth_id // 2 + 1 + step) % 8
+            x = (my_x + 1 + step // 2) % 4
+            half = step % 2
+            block = 2 * x + half
             dens[...] = jnp.dot(lhs[...], ytab[block], preferred_element_type=jnp.float32)
             tiles = [(r, c) for c in range(2) for r in range(2)]
             colour = {t: [jnp.zeros((8, LANES), jnp.float32) for _ in range(3)] for t in tiles}
@@ -192,44 +209,49 @@
                     colour[r, c] = [colour[r, c][q] + weight * value[q] for q in range(3)]
                     clear[r, c] = clear[r, c] - weight
             for c in range(2):
-                d = block * 2 + c
                 for q in range(4):
                     both = jnp.concatenate(
                         [colour[r, c][q] if q < 3 else 1.0 - clear[r, c] for r in range(2)], axis=0
                     )
-                    send2[chunk, d, q] = both.astype(jnp.bfloat16)
-                x, zl = d // 4, d % 4
-                if comm:
-                    @pl.when(d != depth_id)
-                    def _():
-                        pltpu.make_async_remote_copy(
-                            src_ref=send2.at[chunk, d], dst_ref=recv2.at[chunk, depth_id],
-                            send_sem=send_sem.at[CHUNKS + chunk], recv_sem=recv2_sem.at[chunk],
-                            device_id=same_plane(x, zl), device_id_type=MESH,
-                        ).start()
+                    send2[chunk, x, half, q, :, c * LANES : (c + 1) * LANES] = both.astype(jnp.bfloat16)
+            if comm:
+                @pl.when(step < 6)
+                def _():
+                    pltpu.make_async_remote_copy(
+                        src_ref=send2.at[chunk, x, half], dst_ref=recv2.at[chunk, my_x, half],
+                        send_sem=send_sem.at[CHUNKS + chunk], recv_sem=recv2_sem.at[chunk],
+                        device_id=same_plane(x, my_zl), device_id_type=MESH,
+                    ).start()
             return carry
 
         lax.fori_loop(0, 8, columns, 0)
-        recv2[chunk, depth_id] = send2[chunk, depth_id]
-
-    for chunk in range(CHUNKS):
+        recv2[chunk, my_x] = send2[chunk, my_x]
         if comm:
             pltpu.make_async_remote_copy(
-                src_ref=recv2.at[chunk, pl.ds(0, 15)], dst_ref=recv2.at[chunk, pl.ds(0, 15)],
+                src_ref=recv2.at[chunk, pl.ds(0, 3)], dst_ref=recv2.at[chunk, pl.ds(0, 3)],
                 send_sem=send_sem.at[CHUNKS + chunk], recv_sem=recv2_sem.at[chunk],
                 device_id=same_plane((my_x + 1) % 4, my_zl), device_id_type=MESH,
             ).wait_recv()
+        rows = pl.ds(pl.multiple_of(my_zl * 32 + chunk * FINE, FINE), FINE)
         for zl in range(4):
-            rows = slice(zl * 32 + chunk * FINE, zl * 32 + (chunk + 1) * FINE)
-            total = [recv2[chunk, zl, q].astype(jnp.float32) for q in range(3)]
-            clear = 1.0 - recv2[chunk, zl, 3].astype(jnp.float32)
+            half, cols = zl // 2, slice((zl % 2) * LANES, (zl % 2 + 1) * LANES)
+            total = [recv2[chunk, 0, half, q, :, cols].astype(jnp.float32) for q in range(3)]
+            clear = 1.0 - recv2[chunk, 0, half, 3, :, cols].astype(jnp.float32)
             for x in range(1, 4):
                 for q in range(3):
-                    total[q] = total[q] + clear * recv2[chunk, 4 * x + zl, q].astype(jnp.float32)
-                clear = clear * (1.0 - recv2[chunk, 4 * x + zl, 3].astype(jnp.float32))
-            for q in range(3):
-                out_ref[q, rows, :] = total[q]
-            out_ref[3, rows, :] = clear
+                    total[q] = total[q] + clear * recv2[chunk, x, half, q, :, cols].astype(jnp.float32)
+                clear = clear * (1.0 - recv2[chunk, x, half, 3, :, cols].astype(jnp.float32))
+            for q in range(4):
+                send3[chunk, zl, q] = total[q] if q < 3 else clear
+            if comm:
+                @pl.when(my_zl != zl)
+                def _():
+                    pltpu.make_async_remote_copy(
+                        src_ref=send3.at[chunk, zl], dst_ref=out_ref.at[:, rows, :],
+                        send_sem=send_sem.at[2 * CHUNKS + chunk], recv_sem=recv3_sem.at[chunk],
+                        device_id=same_plane(my_x, zl), device_id_type=MESH,
+                    ).start()
+        out_ref[:, rows, :] = send3[chunk, my_zl]
 
     if comm:
         for chunk in range(CHUNKS):
@@ -239,12 +261,19 @@
                 device_id=same_x((my_z + 1) % 8, my_j), device_id_type=MESH,
             ).wait_send()
             pltpu.make_async_remote_copy(
-                src_ref=recv2.at[chunk, pl.ds(0, 15)], dst_ref=recv2.at[chunk, pl.ds(0, 15)],
+                src_ref=recv2.at[chunk, pl.ds(0, 3)], dst_ref=recv2.at[chunk, pl.ds(0, 3)],
                 send_sem=send_sem.at[CHUNKS + chunk], recv_sem=recv2_sem.at[chunk],
                 device_id=same_plane((my_x + 1) % 4, my_zl), device_id_type=MESH,
             ).wait_send()
+            last = pltpu.make_async_remote_copy(
+                src_ref=send3.at[chunk, pl.ds(0, 3)], dst_ref=send3.at[chunk, pl.ds(0, 3)],
+                send_sem=send_sem.at[2 * CHUNKS + chunk], recv_sem=recv3_sem.at[chunk],
+                device_id=same_plane(my_x, (my_zl + 1) % 4), device_id_type=MESH,
+            )
+            last.wait_send()
+            last.wait_recv()
         pltpu.make_async_remote_copy(
-            src_ref=ctab.at[pl.ds(0, 3)], dst_ref=ctab.at[pl.ds(0, 3)], send_sem=send_sem.at[2 * CHUNKS],
+            src_ref=ctab.at[pl.ds(0, 3)], dst_ref=ctab.at[pl.ds(0, 3)], send_sem=send_sem.at[3 * CHUNKS],
             recv_sem=tab_sem, device_id=same_plane(my_x, (my_zl + 1) % 4), device_id_type=MESH,
         ).wait_send()
 
@@ -256,9 +285,14 @@
     return pl.pallas_call(
         functools.partial(kernel, comm=comm),
         out_shape=jax.ShapeDtypeStruct((4, 128, 128), f32),
-        in_specs=[vmem, vmem, pl.BlockSpec(memory_space=pltpu.SMEM), vmem, vmem],
+        in_specs=[pl.BlockSpec(memory_space=pltpu.HBM)] * 5,
         out_specs=vmem,
         scratch_shapes=[
+            pltpu.VMEM((2, 2, 64, NX), bf16),
+            pltpu.VMEM((NMAPS, 4, NCTRL), f32),
+            pltpu.SMEM((2,), jnp.int32),
+            pltpu.VMEM((2, FINE, NX), f32),
+            pltpu.VMEM((2, 128, LANES), f32),
             pltpu.VMEM((256, NX), bf16),
             pltpu.VMEM((128, NX), bf16),
             pltpu.VMEM((128, NX), bf16),
@@ -268,15 +302,18 @@
             pltpu.VMEM((128, NY), bf16),
             pltpu.VMEM((4, 2, 8, LANES), f32),
             pltpu.VMEM((128, 256), f32),
-            pltpu.VMEM((CHUNKS, 16, 4, FINE, LANES), bf16),
-            pltpu.VMEM((CHUNKS, 16, 4, FINE, LANES), bf16),
-            pltpu.SemaphoreType.DMA((2 * CHUNKS + 1,)),
+            pltpu.VMEM((CHUNKS, 4, 2, 4, FINE, 2 * LANES), bf16),
+            pltpu.VMEM((CHUNKS, 4, 2, 4, FINE, 2 * LANES), bf16),
+            pltpu.VMEM((CHUNKS, 4, 4, FINE, LANES), f32),
+            pltpu.SemaphoreType.DMA((5,)),
+            pltpu.SemaphoreType.DMA((3 * CHUNKS + 1,)),
+            pltpu.SemaphoreType.DMA((CHUNKS,)),
             pltpu.SemaphoreType.DMA((CHUNKS,)),
             pltpu.SemaphoreType.DMA((CHUNKS,)),
             pltpu.SemaphoreType.DMA,
         ],
         compiler_params=pltpu.CompilerParams(
-            vmem_limit_bytes=40 << 20,
+            vmem_limit_bytes=60 << 20,
             **(dict(collective_id=0, has_side_effects=True) if comm else {}),
         ),
         name="render",

time: 56.3 us -> 53.3 us (0.947)
  local copies, waits for them, and re-layouts: 5.13 us -> 1.67 us
    unnamed x11 -> x1, local copies, waits for them, and re-layouts: 5.13 us -> 1.67 us
where the time goes in v1:
time: 53.3 us; the launch traced here: 52.8 us
  Pallas kernels  51.1 us (96%)
  local copies, waits for them, and re-layouts  1.67 us (3%)
    pallas_call x1, Pallas kernels, render(): pl.pallas_call(functools.partial(kernel, comm=comm), out_shape=jax.ShapeD...  51.1 us
    unnamed x1, local copies, waits for them, and re-layouts  1.67 us

profile of v1, /device:TPU:1, one launch (start us, length us, event | category | flops | bytes accessed | tf_op | source)
XLA Modules:
  0.0 52.8 jit_solution(8353875863175077508)
XLA Ops:
  0.0 51.1 %render.1 = f32[4,128,128]{2,1,0:T(8,128)} custom-call(bf16[2,2,64,2048]{3,2,1,0:T(8,128)(2,1)} %spec_hbm.1, f32[4,4,16]{2,1,0:T(4,128)} %colour_hbm.1, s32[2]{0:T(128)} %map_hbm.1, f32[2,16,2048]{2,1,0:T(8,128)} %constant.4.clone.fine_hbm, f32[2,128,128]{2,1,0:T(8,128)} %constant.5.clone.coarse_hbm), custom_call_target="tpu_custom_call" | custom-call | tf_op jit(solution)/shard_map/render/pallas_call | solution.py:285
  51.1 1.7 %copy.7 = f32[4,128,128]{2,1,0:T(8,128)} copy(f32[4,128,128]{2,1,0:T(8,128)} %render.1) | data formatting | bytes 524288

commit v2 on v1

v2 whole, which is shorter than its diff:
```python
import functools
import math

import jax
import jax.numpy as jnp
import numpy as np
from jax import lax
from jax.experimental import pallas as pl
from jax.experimental.pallas import tpu as pltpu
from jax.sharding import PartitionSpec as P

NX = 2048
NY = 2048
NCTRL = 16
NMAPS = 4
SPREAD = 3.0
OPACITY = 0.06
LANES = 128
FINE = 16
CHUNKS = 2
MESH = pl.DeviceIdType.MESH


def base_tables():
    fine = 2.0 * np.pi * np.outer(np.arange(FINE), np.arange(NX)) / NX
    coarse = 2.0 * np.pi * (np.outer(np.arange(128), np.arange(128)) % 128) / 128.0
    fine_pair = np.stack([np.cos(fine), np.sin(fine)]).astype(np.float32)
    odd_even = 2.0 * np.pi * np.outer(np.arange(2 * FINE), np.arange(NY // 2)) / NY
    fine_y = np.stack([np.cos(odd_even), np.sin(odd_even)]).reshape(2, FINE, 2, NY // 2)
    fine_y = np.ascontiguousarray(fine_y.transpose(2, 0, 1, 3)).astype(np.float32)
    coarse_pair = np.stack([np.cos(coarse), np.sin(coarse)]).astype(np.float32)
    return fine_pair, fine_y, coarse_pair


def kernel(
    spec_hbm, colour_hbm, map_hbm, fine_hbm, fine_y_hbm, coarse_hbm, out_ref,
    spec_ref, colour_ref, map_ref, fine_ref, fine_y_ref, coarse_ref,
    turned_ref, swapped_ref, cos_ref, sin_ref, send1, recv1, ytab, lhs, ctab, dens, send2, recv2, send3,
    in_sem, send_sem, recv1_sem, recv2_sem, recv3_sem, tab_sem, *, comm
):
    if comm:
        depth_id = lax.axis_index("depth")
        plane_id = lax.axis_index("plane")
    else:
        depth_id = jnp.int32(5)
        plane_id = jnp.int32(6)
    my_x, my_zl = depth_id // 4, depth_id % 4
    my_zh, my_j = plane_id // 8, plane_id % 8
    my_z = my_zh * 4 + my_zl

    fetches = [
        pltpu.make_async_copy(src, dst, in_sem.at[i])
        for i, (src, dst) in enumerate(
            [(spec_hbm, spec_ref), (fine_hbm, fine_ref), (coarse_hbm, coarse_ref),
             (colour_hbm, colour_ref), (map_hbm, map_ref), (fine_y_hbm, fine_y_ref)]
        )
    ]
    for fetch in fetches:
        fetch.start()

    def same_x(z, j):
        return {"depth": my_x * 4 + z % 4, "plane": (z // 4) * 8 + j}

    def same_plane(x, zl):
        return {"depth": x * 4 + zl, "plane": plane_id}

    if comm:
        barrier = pltpu.get_barrier_semaphore()

        def greet_gather(i, carry):
            z, j = (my_z + i // 8) % 8, (my_j + i % 8) % 8
            pl.semaphore_signal(barrier, inc=1, device_id=same_x(z, j), device_id_type=MESH)
            return carry

        def greet_depth(i, carry):
            pl.semaphore_signal(
                barrier, inc=1, device_id=same_plane((my_x + i) % 4, my_zl), device_id_type=MESH
            )
            return carry

        lax.fori_loop(1, 64, greet_gather, 0)
        lax.fori_loop(1, 4, greet_depth, 0)

    for fetch in fetches[:5]:
        fetch.wait()

    source = lax.broadcasted_iota(jnp.int32, (256, 256), 0)
    column = lax.broadcasted_iota(jnp.int32, (256, 256), 1)
    part = (column // 32) % 2
    parity = (column // 64 + plane_id) % 2
    base = (column // 128) * 128 + (column % 32) * 2 + parity
    straight = jnp.where(source == base + 64 * part, 1.0, 0.0).astype(jnp.bfloat16)
    crossed = jnp.where(
        source == base + 64 * (1 - part), jnp.where(part == 0, -1.0, 1.0), 0.0
    ).astype(jnp.bfloat16)
    tn = (((0,), (0,)), ((), ()))
    spec = spec_ref[...].reshape(256, NX)
    turned_ref[...] = lax.dot_general(spec, straight, tn, preferred_element_type=jnp.float32).astype(jnp.bfloat16)
    swapped_ref[...] = lax.dot_general(spec, crossed, tn, preferred_element_type=jnp.float32).astype(jnp.bfloat16)

    for z in range(2):
        values = colour_ref[map_ref[z]]
        values = jnp.concatenate([values, jnp.zeros((4, LANES - NCTRL), jnp.float32)], axis=1)
        row = lax.broadcasted_iota(jnp.int32, (4, LANES), 0)
        values = jnp.where(row == 3, values * OPACITY, values)
        slopes = pltpu.roll(values, LANES - 1, 1) - values
        ctab[my_zl, z] = jnp.concatenate([values, slopes], axis=0)

    x_scale = 1.0 / math.sqrt(NX)
    y_scale = math.sqrt(2.0 / NY)

    def coarse_row(index, scale):
        bc = coarse_ref[0, pl.ds(index, 1), :] * scale
        bs = coarse_ref[1, pl.ds(index, 1), :] * scale
        return jnp.broadcast_to(bc, (FINE, LANES)), jnp.broadcast_to(bs, (FINE, LANES))

    def group_z(k):
        return (my_z + 4 + ((k + 1) // 2) * (1 - 2 * (k % 2))) % 8

    def transform_x(step):
        chunk, k = step // 8, step % 8
        z = group_z(k)
        first = (z // 4) * 64 + 2 * (z % 4) + chunk
        for j in range(8):
            bc, bs = coarse_row(first + 8 * j, x_scale)
            for b in range(NX // LANES):
                cols = slice(b * LANES, (b + 1) * LANES)
                ec, es = fine_ref[0, :, cols], fine_ref[1, :, cols]
                cos_ref[j * FINE : (j + 1) * FINE, cols] = (bc * ec - bs * es).astype(jnp.bfloat16)
                sin_ref[j * FINE : (j + 1) * FINE, cols] = (bs * ec + bc * es).astype(jnp.bfloat16)
        rows = jnp.dot(cos_ref[...], turned_ref[...], preferred_element_type=jnp.float32)
        rows += jnp.dot(sin_ref[...], swapped_ref[...], preferred_element_type=jnp.float32)
        rows = rows.astype(jnp.bfloat16).reshape(8, FINE, 256)
        send1[chunk, k] = rows

    def send_x(step):
        chunk, k = step // 8, step % 8
        z = group_z(k)
        if comm:
            def send(i, c):
                j = (my_j + i) % 8

                @pl.when(jnp.logical_or(k != 7, i != 0))
                def _():
                    pltpu.make_async_remote_copy(
                        src_ref=send1.at[chunk, k, j], dst_ref=recv1.at[chunk, my_zl * 16 + plane_id],
                        send_sem=send_sem.at[chunk], recv_sem=recv1_sem.at[chunk],
                        device_id=same_x(z, j), device_id_type=MESH,
                    ).start()

                return c

            lax.fori_loop(0, 8, send, 0)

    transform_x(0)
    if comm:
        pl.semaphore_wait(barrier, 66)
    send_x(0)
    if comm:
        for k in range(1, 4):
            pltpu.make_async_remote_copy(
                src_ref=ctab.at[my_zl], dst_ref=ctab.at[my_zl], send_sem=send_sem.at[3 * CHUNKS],
                recv_sem=tab_sem, device_id=same_plane(my_x, (my_zl + k) % 4), device_id_type=MESH,
            ).start()

    def x_step(step, carry):
        transform_x(step)
        send_x(step)
        return carry

    lax.fori_loop(1, 8 * CHUNKS, x_step, 0)
    for chunk in range(CHUNKS):
        recv1[chunk, my_zl * 16 + plane_id] = send1[chunk, 7, my_j]
    fetches[5].wait()

    def make_y(i, carry):
        parity, p, quarter = i // 32, (i % 32) // 2, i % 2
        bc, bs = coarse_row(4 * p + 2 * quarter, y_scale)
        base = (p // 2) * LANES + ((p + parity) % 2) * 64 + quarter * FINE
        base = pl.multiple_of(base, FINE)
        for b in range(NY // 2 // LANES):
            cols = slice(b * LANES, (b + 1) * LANES)
            ec, es = fine_y_ref[parity, 0, :, cols], fine_y_ref[parity, 1, :, cols]
            part = slice((b % 2) * LANES, (b % 2 + 1) * LANES)
            ytab[parity, b // 2, pl.ds(base, FINE), part] = (bc * ec - bs * es).astype(jnp.bfloat16)
            ytab[parity, b // 2, pl.ds(base + 32, FINE), part] = (-(bs * ec + bc * es)).astype(jnp.bfloat16)
        return carry

    lax.fori_loop(0, 64, make_y, 0)

    if comm:
        pltpu.make_async_remote_copy(
            src_ref=ctab.at[pl.ds(0, 3)], dst_ref=ctab.at[pl.ds(0, 3)], send_sem=send_sem.at[3 * CHUNKS],
            recv_sem=tab_sem, device_id=same_plane(my_x, (my_zl + 1) % 4), device_id_type=MESH,
        ).wait_recv()

    low = lax.broadcasted_iota(jnp.int32, (FINE, LANES), 1) < 64

    def transform_y(block, slot):
        even = jnp.dot(lhs[0], ytab[0, block], preferred_element_type=jnp.float32)
        odd = jnp.dot(lhs[1], ytab[1, block], preferred_element_type=jnp.float32)
        dens[slot, 0] = even + odd
        dens[slot, 1] = even - odd

    def shade(chunk, x, half, slot, side):
        tiles = [(r, c) for c in range(2) for r in range(2)]
        colour = {t: [jnp.zeros((8, LANES), jnp.float32) for _ in range(3)] for t in tiles}
        clear = {t: jnp.ones((8, LANES), jnp.float32) for t in tiles}
        for z in range(8):
            maps = [jnp.broadcast_to(ctab[z // 2, z % 2, q : q + 1, :], (8, LANES)) for q in range(8)]
            for r, c in tiles:
                d = dens[slot, side, z * FINE + 8 * r : z * FINE + 8 * r + 8, c * LANES : (c + 1) * LANES]
                position = jnp.clip((d + SPREAD) * ((NCTRL - 1) / (2.0 * SPREAD)), 0.0, NCTRL - 1.0)
                index = position.astype(jnp.int32)
                frac = position - index.astype(jnp.float32)
                value = [
                    jnp.take_along_axis(maps[q], index, axis=1, mode="promise_in_bounds")
                    + frac * jnp.take_along_axis(maps[q + 4], index, axis=1, mode="promise_in_bounds")
                    for q in range(4)
                ]
                weight = clear[r, c] * value[3]
                colour[r, c] = [colour[r, c][q] + weight * value[q] for q in range(3)]
                clear[r, c] = clear[r, c] - weight
        for c in range(2):
            for q in range(4):
                both = jnp.concatenate(
                    [colour[r, c][q] if q < 3 else 1.0 - clear[r, c] for r in range(2)], axis=0
                )
                send2[chunk, x, half, q, :, c * LANES : (c + 1) * LANES] = both.astype(jnp.bfloat16)

    def slab(chunk, carry):
        if comm:
            pltpu.make_async_remote_copy(
                src_ref=recv1.at[chunk, pl.ds(0, 63)], dst_ref=recv1.at[chunk, pl.ds(0, 63)],
                send_sem=send_sem.at[chunk], recv_sem=recv1_sem.at[chunk],
                device_id=same_x((my_z + 1) % 8, my_j), device_id_type=MESH,
            ).wait_recv()
        for zl in range(4):
            for z in range(2):
                for pair in range(8):
                    first = recv1[chunk, zl * 16 + 2 * pair, :, z * LANES : (z + 1) * LANES]
                    second = recv1[chunk, zl * 16 + 2 * pair + 1, :, z * LANES : (z + 1) * LANES]
                    rows = slice((2 * zl + z) * FINE, (2 * zl + z + 1) * FINE)
                    cols = slice(pair * LANES, (pair + 1) * LANES)
                    lhs[0, rows, cols] = jnp.where(low, first, second)
                    lhs[1, rows, cols] = jnp.where(low, second, first)

        pairs = [(my_x + 1) % 2, (my_x + 1) % 2, my_x % 2, my_x % 2]
        transform_y(2 * pairs[0], 0)
        for step in range(4):
            half = step % 2
            if step < 3:
                transform_y(2 * pairs[step + 1] + (step + 1) % 2, (step + 1) % 2)
            for side in range(2):
                shade(chunk, pairs[step] + 2 * side, half, step % 2, side)
            if comm:
                for side in range(2):
                    x = pairs[step] + 2 * side

                    @pl.when(x != my_x)
                    def _(x=x, half=half):
                        pltpu.make_async_remote_copy(
                            src_ref=send2.at[chunk, x, half], dst_ref=recv2.at[chunk, my_x, half],
                            send_sem=send_sem.at[CHUNKS + chunk], recv_sem=recv2_sem.at[chunk],
                            device_id=same_plane(x, my_zl), device_id_type=MESH,
                        ).start()

        recv2[chunk, my_x] = send2[chunk, my_x]
        if comm:
            pltpu.make_async_remote_copy(
                src_ref=recv2.at[chunk, pl.ds(0, 3)], dst_ref=recv2.at[chunk, pl.ds(0, 3)],
                send_sem=send_sem.at[CHUNKS + chunk], recv_sem=recv2_sem.at[chunk],
                device_id=same_plane((my_x + 1) % 4, my_zl), device_id_type=MESH,
            ).wait_recv()
        rows = pl.ds(pl.multiple_of(my_zl * 32 + chunk * FINE, FINE), FINE)
        for zl in range(4):
            half, cols = zl // 2, slice((zl % 2) * LANES, (zl % 2 + 1) * LANES)
            total = [recv2[chunk, 0, half, q, :, cols].astype(jnp.float32) for q in range(3)]
            clear = 1.0 - recv2[chunk, 0, half, 3, :, cols].astype(jnp.float32)
            for x in range(1, 4):
                for q in range(3):
                    total[q] = total[q] + clear * recv2[chunk, x, half, q, :, cols].astype(jnp.float32)
                clear = clear * (1.0 - recv2[chunk, x, half, 3, :, cols].astype(jnp.float32))
            for q in range(4):
                send3[chunk, zl, q] = total[q] if q < 3 else clear
            if comm:
                @pl.when(my_zl != zl)
                def _(zl=zl):
                    pltpu.make_async_remote_copy(
                        src_ref=send3.at[chunk, zl], dst_ref=out_ref.at[:, rows, :],
                        send_sem=send_sem.at[2 * CHUNKS + chunk], recv_sem=recv3_sem.at[chunk],
                        device_id=same_plane(my_x, zl), device_id_type=MESH,
                    ).start()
        out_ref[:, rows, :] = send3[chunk, my_zl]
        return carry

    lax.fori_loop(0, CHUNKS, slab, 0)

    if comm:
        for chunk in range(CHUNKS):
            pltpu.make_async_remote_copy(
                src_ref=recv1.at[chunk, pl.ds(0, 63)], dst_ref=recv1.at[chunk, pl.ds(0, 63)],
                send_sem=send_sem.at[chunk], recv_sem=recv1_sem.at[chunk],
                device_id=same_x((my_z + 1) % 8, my_j), device_id_type=MESH,
            ).wait_send()
            pltpu.make_async_remote_copy(
                src_ref=recv2.at[chunk, pl.ds(0, 3)], dst_ref=recv2.at[chunk, pl.ds(0, 3)],
                send_sem=send_sem.at[CHUNKS + chunk], recv_sem=recv2_sem.at[chunk],
                device_id=same_plane((my_x + 1) % 4, my_zl), device_id_type=MESH,
            ).wait_send()
            last = pltpu.make_async_remote_copy(
                src_ref=send3.at[chunk, pl.ds(0, 3)], dst_ref=send3.at[chunk, pl.ds(0, 3)],
                send_sem=send_sem.at[2 * CHUNKS + chunk], recv_sem=recv3_sem.at[chunk],
                device_id=same_plane(my_x, (my_zl + 1) % 4), device_id_type=MESH,
            )
            last.wait_send()
            last.wait_recv()
        pltpu.make_async_remote_copy(
            src_ref=ctab.at[pl.ds(0, 3)], dst_ref=ctab.at[pl.ds(0, 3)], send_sem=send_sem.at[3 * CHUNKS],
            recv_sem=tab_sem, device_id=same_plane(my_x, (my_zl + 1) % 4), device_id_type=MESH,
        ).wait_send()


def render(spectrum, colour_table, map_index, comm=True):
    fine_pair, fine_y, coarse_pair = base_tables()
    vmem = pl.BlockSpec(memory_space=pltpu.VMEM)
    bf16, f32 = jnp.bfloat16, jnp.float32
    return pl.pallas_call(
        functools.partial(kernel, comm=comm),
        out_shape=jax.ShapeDtypeStruct((4, 128, 128), f32),
        in_specs=[pl.BlockSpec(memory_space=pltpu.HBM)] * 6,
        out_specs=vmem,
        scratch_shapes=[
            pltpu.VMEM((2, 2, 64, NX), bf16),
            pltpu.VMEM((NMAPS, 4, NCTRL), f32),
            pltpu.SMEM((2,), jnp.int32),
            pltpu.VMEM((2, FINE, NX), f32),
            pltpu.VMEM((2, 2, FINE, NY // 2), f32),
            pltpu.VMEM((2, 128, LANES), f32),
            pltpu.VMEM((NX, 256), bf16),
            pltpu.VMEM((NX, 256), bf16),
            pltpu.VMEM((128, NX), bf16),
            pltpu.VMEM((128, NX), bf16),
            pltpu.VMEM((CHUNKS, 8, 8, FINE, 256), bf16),
            pltpu.VMEM((CHUNKS, 64, FINE, 256), bf16),
            pltpu.VMEM((2, 4, NY // 2, 256), bf16),
            pltpu.VMEM((2, 128, NY // 2), bf16),
            pltpu.VMEM((4, 2, 8, LANES), f32),
            pltpu.VMEM((2, 2, 128, 256), f32),
            pltpu.VMEM((CHUNKS, 4, 2, 4, FINE, 2 * LANES), bf16),
            pltpu.VMEM((CHUNKS, 4, 2, 4, FINE, 2 * LANES), bf16),
            pltpu.VMEM((CHUNKS, 4, 4, FINE, LANES), f32),
            pltpu.SemaphoreType.DMA((6,)),
            pltpu.SemaphoreType.DMA((3 * CHUNKS + 1,)),
            pltpu.SemaphoreType.DMA((CHUNKS,)),
            pltpu.SemaphoreType.DMA((CHUNKS,)),
            pltpu.SemaphoreType.DMA((CHUNKS,)),
            pltpu.SemaphoreType.DMA,
        ],
        compiler_params=pltpu.CompilerParams(
            vmem_limit_bytes=60 << 20,
            **(dict(collective_id=0, has_side_effects=True) if comm else {}),
        ),
        name="render",
    )(spectrum, colour_table, map_index, jnp.asarray(fine_pair), jnp.asarray(fine_y), jnp.asarray(coarse_pair))


def solution(mesh):
    return jax.shard_map(
        render,
        mesh=mesh,
        in_specs=(P("depth", None, "plane", None), P(), P("depth")),
        out_specs=P(None, "plane", "depth"),
        check_vma=False,
    )
```

time: 53.3 us -> 51.9 us (0.974)
  Pallas kernels: 51.1 us -> 50.1 us
    pallas_call x1, Pallas kernels: 51.1 us -> 50.1 us  [render(): pl.pallas_call(functools.partial(kernel, comm=comm), out_shape=jax.ShapeD...]
where the time goes in v2:
time: 51.9 us; the launch traced here: 51.8 us
  Pallas kernels  50.1 us (97%)
  local copies, waits for them, and re-layouts  1.67 us (3%)
    pallas_call x1, Pallas kernels, render(): pl.pallas_call(functools.partial(kernel, comm=comm), out_shape=jax.ShapeD...  50.1 us
    unnamed x1, local copies, waits for them, and re-layouts  1.67 us

profile of v2, /device:TPU:1, one launch (start us, length us, event | category | flops | bytes accessed | tf_op | source)
XLA Modules:
  0.0 51.8 jit_solution(5496825022665550670)
XLA Ops:
  0.0 50.1 %render.1 = f32[4,128,128]{2,1,0:T(8,128)} custom-call(bf16[2,2,64,2048]{3,2,1,0:T(8,128)(2,1)} %spec_hbm.1, f32[4,4,16]{2,1,0:T(4,128)} %colour_hbm.1, s32[2]{0:T(128)} %map_hbm.1, f32[2,16,2048]{2,1,0:T(8,128)} %constant.6.clone.fine_hbm, f32[2,2,16,1024]{3,2,1,0:T(8,128)} %constant.7.clone.fine_y_hbm, f32[2,128,128]{2,1,0:T(8,128)} %constant.8.clone.coarse_hbm), custom_call_target="tpu_custom_call" | custom-call | tf_op jit(solution)/shard_map/render/pallas_call | solution.py:328
  50.1 1.7 %copy.8 = f32[4,128,128]{2,1,0:T(8,128)} copy(f32[4,128,128]{2,1,0:T(8,128)} %render.1) | data formatting | bytes 524288

commit v3 on v2

--- a/solution.py
+++ b/solution.py
@@ -114,40 +114,42 @@
         bs = coarse_ref[1, pl.ds(index, 1), :] * scale
         return jnp.broadcast_to(bc, (FINE, LANES)), jnp.broadcast_to(bs, (FINE, LANES))
 
-    def group_z(k):
-        return (my_z + 4 + ((k + 1) // 2) * (1 - 2 * (k % 2))) % 8
+    def pair_z(k):
+        return (my_z + 4 - k) % 8, (my_z + 4 + k + 4 * ((4 - k) // 4)) % 8
 
     def transform_x(step):
-        chunk, k = step // 8, step % 8
-        z = group_z(k)
-        first = (z // 4) * 64 + 2 * (z % 4) + chunk
-        for j in range(8):
-            bc, bs = coarse_row(first + 8 * j, x_scale)
-            for b in range(NX // LANES):
-                cols = slice(b * LANES, (b + 1) * LANES)
-                ec, es = fine_ref[0, :, cols], fine_ref[1, :, cols]
-                cos_ref[j * FINE : (j + 1) * FINE, cols] = (bc * ec - bs * es).astype(jnp.bfloat16)
-                sin_ref[j * FINE : (j + 1) * FINE, cols] = (bs * ec + bc * es).astype(jnp.bfloat16)
+        chunk, k = step // 4, step % 4
+        for i, z in enumerate(pair_z(k)):
+            first = (z // 4) * 64 + 2 * (z % 4) + chunk
+            for j in range(8):
+                bc, bs = coarse_row(first + 8 * j, x_scale)
+                rows = slice((8 * i + j) * FINE, (8 * i + j + 1) * FINE)
+                for b in range(NX // LANES):
+                    cols = slice(b * LANES, (b + 1) * LANES)
+                    ec, es = fine_ref[0, :, cols], fine_ref[1, :, cols]
+                    cos_ref[rows, cols] = (bc * ec - bs * es).astype(jnp.bfloat16)
+                    sin_ref[rows, cols] = (bs * ec + bc * es).astype(jnp.bfloat16)
         rows = jnp.dot(cos_ref[...], turned_ref[...], preferred_element_type=jnp.float32)
         rows += jnp.dot(sin_ref[...], swapped_ref[...], preferred_element_type=jnp.float32)
-        rows = rows.astype(jnp.bfloat16).reshape(8, FINE, 256)
+        rows = rows.astype(jnp.bfloat16).reshape(2, 8, FINE, 256)
         send1[chunk, k] = rows
 
     def send_x(step):
-        chunk, k = step // 8, step % 8
-        z = group_z(k)
+        chunk, k = step // 4, step % 4
+        zs = pair_z(k)
         if comm:
             def send(i, c):
                 j = (my_j + i) % 8
-
-                @pl.when(jnp.logical_or(k != 7, i != 0))
-                def _():
-                    pltpu.make_async_remote_copy(
-                        src_ref=send1.at[chunk, k, j], dst_ref=recv1.at[chunk, my_zl * 16 + plane_id],
+                for side, z in enumerate(zs):
+                    copy = pltpu.make_async_remote_copy(
+                        src_ref=send1.at[chunk, k, side, j], dst_ref=recv1.at[chunk, my_zl * 16 + plane_id],
                         send_sem=send_sem.at[chunk], recv_sem=recv1_sem.at[chunk],
                         device_id=same_x(z, j), device_id_type=MESH,
-                    ).start()
-
+                    )
+                    if side == 0:
+                        copy.start()
+                    else:
+                        pl.when(jnp.logical_or(k != 0, i != 0))(copy.start)
                 return c
 
             lax.fori_loop(0, 8, send, 0)
@@ -168,9 +170,9 @@
         send_x(step)
         return carry
 
-    lax.fori_loop(1, 8 * CHUNKS, x_step, 0)
+    lax.fori_loop(1, 4 * CHUNKS, x_step, 0)
     for chunk in range(CHUNKS):
-        recv1[chunk, my_zl * 16 + plane_id] = send1[chunk, 7, my_j]
+        recv1[chunk, my_zl * 16 + plane_id] = send1[chunk, 0, 1, my_j]
     fetches[5].wait()
 
     def make_y(i, carry):
@@ -196,20 +198,23 @@
 
     low = lax.broadcasted_iota(jnp.int32, (FINE, LANES), 1) < 64
 
-    def transform_y(block, slot):
-        even = jnp.dot(lhs[0], ytab[0, block], preferred_element_type=jnp.float32)
-        odd = jnp.dot(lhs[1], ytab[1, block], preferred_element_type=jnp.float32)
-        dens[slot, 0] = even + odd
-        dens[slot, 1] = even - odd
-
-    def shade(chunk, x, half, slot, side):
+    def transform_y(block, slot, piece):
+        parity, depth = piece // 4, slice((piece % 4) * 256, (piece % 4 + 1) * 256)
+        part = jnp.dot(lhs[parity, :, depth], ytab[parity, block, depth, :], preferred_element_type=jnp.float32)
+        dens[slot, parity] = part if piece % 4 == 0 else dens[slot, parity] + part
+
+    def shade(chunk, x, half, slot, side, following):
         tiles = [(r, c) for c in range(2) for r in range(2)]
         colour = {t: [jnp.zeros((8, LANES), jnp.float32) for _ in range(3)] for t in tiles}
         clear = {t: jnp.ones((8, LANES), jnp.float32) for t in tiles}
         for z in range(8):
+            if following is not None and z % 2 == 0:
+                transform_y(*following, 4 * side + z // 2)
             maps = [jnp.broadcast_to(ctab[z // 2, z % 2, q : q + 1, :], (8, LANES)) for q in range(8)]
             for r, c in tiles:
-                d = dens[slot, side, z * FINE + 8 * r : z * FINE + 8 * r + 8, c * LANES : (c + 1) * LANES]
+                at = (slice(z * FINE + 8 * r, z * FINE + 8 * r + 8), slice(c * LANES, (c + 1) * LANES))
+                even, odd = dens[(slot, 0, *at)], dens[(slot, 1, *at)]
+                d = even - odd if side else even + odd
                 position = jnp.clip((d + SPREAD) * ((NCTRL - 1) / (2.0 * SPREAD)), 0.0, NCTRL - 1.0)
                 index = position.astype(jnp.int32)
                 frac = position - index.astype(jnp.float32)
@@ -246,13 +251,13 @@
                     lhs[1, rows, cols] = jnp.where(low, second, first)
 
         pairs = [(my_x + 1) % 2, (my_x + 1) % 2, my_x % 2, my_x % 2]
-        transform_y(2 * pairs[0], 0)
+        for piece in range(8):
+            transform_y(2 * pairs[0], 0, piece)
         for step in range(4):
             half = step % 2
-            if step < 3:
-                transform_y(2 * pairs[step + 1] + (step + 1) % 2, (step + 1) % 2)
+            following = (2 * pairs[step + 1] + (step + 1) % 2, (step + 1) % 2) if step < 3 else None
             for side in range(2):
-                shade(chunk, pairs[step] + 2 * side, half, step % 2, side)
+                shade(chunk, pairs[step] + 2 * side, half, step % 2, side, following)
             if comm:
                 for side in range(2):
                     x = pairs[step] + 2 * side
@@ -339,9 +344,9 @@
             pltpu.VMEM((2, 128, LANES), f32),
             pltpu.VMEM((NX, 256), bf16),
             pltpu.VMEM((NX, 256), bf16),
-            pltpu.VMEM((128, NX), bf16),
-            pltpu.VMEM((128, NX), bf16),
-            pltpu.VMEM((CHUNKS, 8, 8, FINE, 256), bf16),
+            pltpu.VMEM((256, NX), bf16),
+            pltpu.VMEM((256, NX), bf16),
+            pltpu.VMEM((CHUNKS, 4, 2, 8, FINE, 256), bf16),
             pltpu.VMEM((CHUNKS, 64, FINE, 256), bf16),
             pltpu.VMEM((2, 4, NY // 2, 256), bf16),
             pltpu.VMEM((2, 128, NY // 2), bf16),

time: 51.9 us -> 51.9 us (level)
  no operation moved by 1% of the time
where the time goes in v3:
time: 51.9 us; the launch traced here: 51.8 us
  Pallas kernels  50.1 us (97%)
  local copies, waits for them, and re-layouts  1.67 us (3%)
    pallas_call x1, Pallas kernels, render(): pl.pallas_call(functools.partial(kernel, comm=comm), out_shape=jax.ShapeD...  50.1 us
    unnamed x1, local copies, waits for them, and re-layouts  1.67 us

profile of v3, /device:TPU:1, one launch (start us, length us, event | category | flops | bytes accessed | tf_op | source)
XLA Modules:
  0.0 51.8 jit_solution(11524512282497531303)
XLA Ops:
  0.0 50.1 %render.1 = f32[4,128,128]{2,1,0:T(8,128)} custom-call(bf16[2,2,64,2048]{3,2,1,0:T(8,128)(2,1)} %spec_hbm.1, f32[4,4,16]{2,1,0:T(4,128)} %colour_hbm.1, s32[2]{0:T(128)} %map_hbm.1, f32[2,16,2048]{2,1,0:T(8,128)} %constant.6.clone.fine_hbm, f32[2,2,16,1024]{3,2,1,0:T(8,128)} %constant.7.clone.fine_y_hbm, f32[2,128,128]{2,1,0:T(8,128)} %constant.8.clone.coarse_hbm), custom_call_target="tpu_custom_call" | custom-call | tf_op jit(solution)/shard_map/render/pallas_call | solution.py:333
  50.1 1.7 %copy.8 = f32[4,128,128]{2,1,0:T(8,128)} copy(f32[4,128,128]{2,1,0:T(8,128)} %render.1) | data formatting | bytes 524288

commit v4 on v3

v4 whole, which is shorter than its diff:
```python
import functools
import math

import jax
import jax.numpy as jnp
import numpy as np
from jax import lax
from jax.experimental import pallas as pl
from jax.experimental.pallas import tpu as pltpu
from jax.sharding import PartitionSpec as P

NX = 2048
NY = 2048
NCTRL = 16
NMAPS = 4
SPREAD = 3.0
OPACITY = 0.06
LANES = 128
FINE = 16
OCTETS = 4
OCT = 8
MESH = pl.DeviceIdType.MESH


def base_tables():
    fine = 2.0 * np.pi * np.outer(np.arange(FINE), np.arange(NX)) / NX
    coarse = 2.0 * np.pi * (np.outer(np.arange(128), np.arange(128)) % 128) / 128.0
    fine_pair = np.stack([np.cos(fine), np.sin(fine)]).astype(np.float32)
    odd_even = 2.0 * np.pi * np.outer(np.arange(2 * FINE), np.arange(NY // 2)) / NY
    fine_y = np.stack([np.cos(odd_even), np.sin(odd_even)]).reshape(2, FINE, 2, NY // 2)
    fine_y = np.ascontiguousarray(fine_y.transpose(2, 0, 1, 3)).astype(np.float32)
    coarse_pair = np.stack([np.cos(coarse), np.sin(coarse)]).astype(np.float32)
    return fine_pair, fine_y, coarse_pair


def kernel(
    spec_hbm, colour_hbm, map_hbm, fine_hbm, fine_y_hbm, coarse_hbm, out_ref,
    spec_ref, colour_ref, map_ref, fine_ref, fine_y_ref, coarse_ref,
    turned_ref, swapped_ref, cos_ref, sin_ref, send1, recv1, ytab, lhs, ctab, dens, send2, recv2, send3,
    in_sem, send_sem, recv1_sem, recv2_sem, recv3_sem, tab_sem, *, comm
):
    if comm:
        depth_id = lax.axis_index("depth")
        plane_id = lax.axis_index("plane")
    else:
        depth_id = jnp.int32(5)
        plane_id = jnp.int32(6)
    my_x, my_zl = depth_id // 4, depth_id % 4
    my_zh, my_j = plane_id // 8, plane_id % 8
    my_z = my_zh * 4 + my_zl

    fetches = [
        pltpu.make_async_copy(src, dst, in_sem.at[i])
        for i, (src, dst) in enumerate(
            [(spec_hbm, spec_ref), (fine_hbm, fine_ref), (coarse_hbm, coarse_ref),
             (colour_hbm, colour_ref), (map_hbm, map_ref), (fine_y_hbm, fine_y_ref)]
        )
    ]
    for fetch in fetches:
        fetch.start()

    def same_x(z, j):
        return {"depth": my_x * 4 + z % 4, "plane": (z // 4) * 8 + j}

    def same_plane(x, zl):
        return {"depth": x * 4 + zl, "plane": plane_id}

    if comm:
        barrier = pltpu.get_barrier_semaphore()

        def greet_gather(i, carry):
            z, j = (my_z + i // 8) % 8, (my_j + i % 8) % 8
            pl.semaphore_signal(barrier, inc=1, device_id=same_x(z, j), device_id_type=MESH)
            return carry

        def greet_depth(i, carry):
            pl.semaphore_signal(
                barrier, inc=1, device_id=same_plane((my_x + i) % 4, my_zl), device_id_type=MESH
            )
            return carry

        lax.fori_loop(1, 64, greet_gather, 0)
        lax.fori_loop(1, 4, greet_depth, 0)

    x_scale = 1.0 / math.sqrt(NX)
    y_scale = math.sqrt(2.0 / NY)

    def coarse_row(index, scale):
        bc = coarse_ref[0, pl.ds(index, 1), :] * scale
        bs = coarse_ref[1, pl.ds(index, 1), :] * scale
        return jnp.broadcast_to(bc, (FINE, LANES)), jnp.broadcast_to(bs, (FINE, LANES))

    def pair_z(k):
        return (my_z + 4 - k) % 8, (my_z + 4 + k + 4 * ((4 - k) // 4)) % 8

    def x_tables(chunk, k):
        for i, z in enumerate(pair_z(k)):
            first = (z // 4) * 64 + 2 * (z % 4) + chunk
            for j in range(8):
                bc, bs = coarse_row(first + 8 * j, x_scale)
                rows = slice((8 * i + j) * FINE, (8 * i + j + 1) * FINE)
                for b in range(NX // LANES):
                    cols = slice(b * LANES, (b + 1) * LANES)
                    ec, es = fine_ref[0, :, cols], fine_ref[1, :, cols]
                    cos_ref[rows, cols] = (bc * ec - bs * es).astype(jnp.bfloat16)
                    sin_ref[rows, cols] = (bs * ec + bc * es).astype(jnp.bfloat16)

    def x_rows(chunk, k):
        rows = jnp.dot(cos_ref[...], turned_ref[...], preferred_element_type=jnp.float32)
        rows += jnp.dot(sin_ref[...], swapped_ref[...], preferred_element_type=jnp.float32)
        send1[chunk, k] = rows.reshape(2, 8, 2, OCT, 256).astype(jnp.bfloat16)

    def send_x(k, part):
        zs = pair_z(k)
        if not comm:
            return

        def send(i, c):
            j = (my_j + i) % 8
            for side, z in enumerate(zs):
                if part == 0:
                    src, dst = send1.at[0, k, side, j], recv1.at[0, my_zl * 16 + plane_id]
                else:
                    src = send1.at[1, k, side, j, part - 1]
                    dst = recv1.at[1, my_zl * 16 + plane_id, part - 1]
                copy = pltpu.make_async_remote_copy(
                    src_ref=src, dst_ref=dst, send_sem=send_sem.at[0], recv_sem=recv1_sem.at[part],
                    device_id=same_x(z, j), device_id_type=MESH,
                )
                if side == 0:
                    copy.start()
                else:
                    pl.when(jnp.logical_or(k != 0, i != 0))(copy.start)
            return c

        lax.fori_loop(0, 8, send, 0)

    fetches[1].wait()
    fetches[2].wait()
    x_tables(0, 0)
    fetches[0].wait()

    source = lax.broadcasted_iota(jnp.int32, (256, 256), 0)
    column = lax.broadcasted_iota(jnp.int32, (256, 256), 1)
    part = (column // 32) % 2
    parity = (column // 64 + plane_id) % 2
    base = (column // 128) * 128 + (column % 32) * 2 + parity
    straight = jnp.where(source == base + 64 * part, 1.0, 0.0).astype(jnp.bfloat16)
    crossed = jnp.where(
        source == base + 64 * (1 - part), jnp.where(part == 0, -1.0, 1.0), 0.0
    ).astype(jnp.bfloat16)
    tn = (((0,), (0,)), ((), ()))
    spec = spec_ref[...].reshape(256, NX)
    turned_ref[...] = lax.dot_general(spec, straight, tn, preferred_element_type=jnp.float32).astype(jnp.bfloat16)
    swapped_ref[...] = lax.dot_general(spec, crossed, tn, preferred_element_type=jnp.float32).astype(jnp.bfloat16)

    x_rows(0, 0)
    fetches[3].wait()
    fetches[4].wait()

    for z in range(2):
        values = colour_ref[map_ref[z]]
        values = jnp.concatenate([values, jnp.zeros((4, LANES - NCTRL), jnp.float32)], axis=1)
        row = lax.broadcasted_iota(jnp.int32, (4, LANES), 0)
        values = jnp.where(row == 3, values * OPACITY, values)
        slopes = pltpu.roll(values, LANES - 1, 1) - values
        ctab[my_zl, z] = jnp.concatenate([values, slopes], axis=0)

    if comm:
        pl.semaphore_wait(barrier, 66)
    send_x(0, 0)
    if comm:
        for k in range(1, 4):
            pltpu.make_async_remote_copy(
                src_ref=ctab.at[my_zl], dst_ref=ctab.at[my_zl], send_sem=send_sem.at[3],
                recv_sem=tab_sem, device_id=same_plane(my_x, (my_zl + k) % 4), device_id_type=MESH,
            ).start()

    def first_half(k, carry):
        x_tables(0, k)
        x_rows(0, k)
        send_x(k, 0)
        return carry

    def second_half(k, carry):
        x_tables(1, k)
        x_rows(1, k)
        send_x(k, 1)
        return carry

    def last_part(k, carry):
        send_x(k, 2)
        return carry

    lax.fori_loop(1, 4, first_half, 0)
    lax.fori_loop(0, 4, second_half, 0)
    lax.fori_loop(0, 4, last_part, 0)
    for chunk in range(2):
        recv1[chunk, my_zl * 16 + plane_id] = send1[chunk, 0, 1, my_j]
    fetches[5].wait()

    def make_y(i, carry):
        parity, p, quarter = i // 32, (i % 32) // 2, i % 2
        bc, bs = coarse_row(4 * p + 2 * quarter, y_scale)
        base = (p // 2) * LANES + ((p + parity) % 2) * 64 + quarter * FINE
        base = pl.multiple_of(base, FINE)
        for b in range(NY // 2 // LANES):
            cols = slice(b * LANES, (b + 1) * LANES)
            ec, es = fine_y_ref[parity, 0, :, cols], fine_y_ref[parity, 1, :, cols]
            part = slice((b % 2) * LANES, (b % 2 + 1) * LANES)
            ytab[parity, b // 2, pl.ds(base, FINE), part] = (bc * ec - bs * es).astype(jnp.bfloat16)
            ytab[parity, b // 2, pl.ds(base + 32, FINE), part] = (-(bs * ec + bc * es)).astype(jnp.bfloat16)
        return carry

    lax.fori_loop(0, 64, make_y, 0)

    def table_copy():
        return pltpu.make_async_remote_copy(
            src_ref=ctab.at[pl.ds(0, 3)], dst_ref=ctab.at[pl.ds(0, 3)], send_sem=send_sem.at[3],
            recv_sem=tab_sem, device_id=same_plane(my_x, (my_zl + 1) % 4), device_id_type=MESH,
        )

    def waiting(ref, send_slot, recv, device):
        return pltpu.make_async_remote_copy(
            src_ref=ref, dst_ref=ref, send_sem=send_sem.at[send_slot], recv_sem=recv,
            device_id=device, device_id_type=MESH,
        )

    next_z = same_x((my_z + 1) % 8, my_j)
    next_x = same_plane((my_x + 1) % 4, my_zl)
    next_zl = same_plane(my_x, (my_zl + 1) % 4)
    if comm:
        table_copy().wait_recv()

    low = lax.broadcasted_iota(jnp.int32, (OCT, LANES), 1) < 64

    def transform_y(block, slot, piece):
        parity, depth = piece // 4, slice((piece % 4) * 256, (piece % 4 + 1) * 256)
        part = jnp.dot(lhs[parity, :, depth], ytab[parity, block, depth, :], preferred_element_type=jnp.float32)
        dens[slot, parity] = part if piece % 4 == 0 else dens[slot, parity] + part

    def shade(octet, xs, half, slot, following):
        tiles = [(i, c) for i in range(len(xs)) for c in range(2)]
        signs = [(1 - 2 * (x // 2)).astype(jnp.float32) for x in xs]
        colour = {t: [jnp.zeros((OCT, LANES), jnp.float32) for _ in range(3)] for t in tiles}
        clear = {t: jnp.ones((OCT, LANES), jnp.float32) for t in tiles}
        for z in range(8):
            if following is not None:
                transform_y(*following, z)
            maps = [jnp.broadcast_to(ctab[z // 2, z % 2, q : q + 1, :], (OCT, LANES)) for q in range(8)]
            for t in tiles:
                i, c = t
                at = (slice(z * OCT, (z + 1) * OCT), slice(c * LANES, (c + 1) * LANES))
                d = dens[(slot, 0, *at)] + signs[i] * dens[(slot, 1, *at)]
                position = jnp.clip((d + SPREAD) * ((NCTRL - 1) / (2.0 * SPREAD)), 0.0, NCTRL - 1.0)
                index = position.astype(jnp.int32)
                frac = position - index.astype(jnp.float32)
                value = [
                    jnp.take_along_axis(maps[q], index, axis=1, mode="promise_in_bounds")
                    + frac * jnp.take_along_axis(maps[q + 4], index, axis=1, mode="promise_in_bounds")
                    for q in range(4)
                ]
                weight = clear[t] * value[3]
                colour[t] = [colour[t][q] + weight * value[q] for q in range(3)]
                clear[t] = clear[t] - weight
        for i, c in tiles:
            for q in range(4):
                result = colour[i, c][q] if q < 3 else 1.0 - clear[i, c]
                send2[octet, xs[i], half, q, :, c * LANES : (c + 1) * LANES] = result.astype(jnp.bfloat16)

    def send_x_part(octet, x, half):
        if comm:
            pltpu.make_async_remote_copy(
                src_ref=send2.at[octet, x, half], dst_ref=recv2.at[octet, my_x, half],
                send_sem=send_sem.at[1], recv_sem=recv2_sem.at[octet],
                device_id=same_plane(x, my_zl), device_id_type=MESH,
            ).start()

    def combine(octet):
        if comm:
            waiting(recv2.at[octet, pl.ds(0, 3)], 1, recv2_sem.at[octet], next_x).wait_recv()
        rows = pl.ds(pl.multiple_of(my_zl * 32 + octet * OCT, OCT), OCT)
        for zl in range(4):
            half, cols = zl // 2, slice((zl % 2) * LANES, (zl % 2 + 1) * LANES)
            total = [recv2[octet, 0, half, q, :, cols].astype(jnp.float32) for q in range(3)]
            clear = 1.0 - recv2[octet, 0, half, 3, :, cols].astype(jnp.float32)
            for x in range(1, 4):
                for q in range(3):
                    total[q] = total[q] + clear * recv2[octet, x, half, q, :, cols].astype(jnp.float32)
                clear = clear * (1.0 - recv2[octet, x, half, 3, :, cols].astype(jnp.float32))
            for q in range(4):
                send3[octet, zl, q] = total[q] if q < 3 else clear
            if comm:
                @pl.when(my_zl != zl)
                def _(zl=zl):
                    pltpu.make_async_remote_copy(
                        src_ref=send3.at[octet, zl], dst_ref=out_ref.at[:, rows, :],
                        send_sem=send_sem.at[2], recv_sem=recv3_sem,
                        device_id=same_plane(my_x, zl), device_id_type=MESH,
                    ).start()
        out_ref[:, rows, :] = send3[octet, my_zl]

    def slab(octet, carry):
        chunk, part = octet // 2, octet % 2
        if comm:
            @pl.when(octet == 0)
            def _():
                waiting(recv1.at[0, pl.ds(0, 63)], 0, recv1_sem.at[0], next_z).wait_recv()

            for half in range(2):
                @pl.when(octet == 2 + half)
                def _(half=half):
                    waiting(recv1.at[1, pl.ds(0, 63), half], 0, recv1_sem.at[1 + half], next_z).wait_recv()

        for zl in range(4):
            for z in range(2):
                for pair in range(8):
                    first = recv1[chunk, zl * 16 + 2 * pair, part, :, z * LANES : (z + 1) * LANES]
                    second = recv1[chunk, zl * 16 + 2 * pair + 1, part, :, z * LANES : (z + 1) * LANES]
                    rows = slice((2 * zl + z) * OCT, (2 * zl + z + 1) * OCT)
                    cols = slice(pair * LANES, (pair + 1) * LANES)
                    lhs[0, rows, cols] = jnp.where(low, first, second)
                    lhs[1, rows, cols] = jnp.where(low, second, first)

        theirs = 2 * ((my_x + 1) % 2)
        ours = 2 * (my_x % 2)
        others = [(my_x + 1) % 4, (my_x + 3) % 4]
        across = (my_x + 2) % 4
        for piece in range(8):
            transform_y(theirs, 0, piece)
        shade(octet, others, 0, 0, (theirs + 1, 1))
        for x in others:
            send_x_part(octet, x, 0)
        shade(octet, others, 1, 1, (ours, 0))
        for x in others:
            send_x_part(octet, x, 1)
        shade(octet, [across], 0, 0, (ours + 1, 1))
        send_x_part(octet, across, 0)
        shade(octet, [across], 1, 1, None)
        send_x_part(octet, across, 1)
        shade(octet, [my_x], 0, 0, None)
        shade(octet, [my_x], 1, 1, None)
        recv2[octet, my_x] = send2[octet, my_x]

        @pl.when(octet > 0)
        def _():
            combine(octet - 1)

        return carry

    lax.fori_loop(0, OCTETS, slab, 0)
    combine(OCTETS - 1)

    if comm:
        waiting(recv1.at[:, pl.ds(0, 63)], 0, recv1_sem.at[0], next_z).wait_send()
        waiting(recv2.at[:, pl.ds(0, 3)], 1, recv2_sem.at[0], next_x).wait_send()
        last = waiting(send3.at[pl.ds(0, 3)], 2, recv3_sem, next_zl)
        last.wait_send()
        last.wait_recv()
        table_copy().wait_send()


def render(spectrum, colour_table, map_index, comm=True):
    fine_pair, fine_y, coarse_pair = base_tables()
    vmem = pl.BlockSpec(memory_space=pltpu.VMEM)
    bf16, f32 = jnp.bfloat16, jnp.float32
    return pl.pallas_call(
        functools.partial(kernel, comm=comm),
        out_shape=jax.ShapeDtypeStruct((4, 128, 128), f32),
        in_specs=[pl.BlockSpec(memory_space=pltpu.HBM)] * 6,
        out_specs=vmem,
        scratch_shapes=[
            pltpu.VMEM((2, 2, 64, NX), bf16),
            pltpu.VMEM((NMAPS, 4, NCTRL), f32),
            pltpu.SMEM((2,), jnp.int32),
            pltpu.VMEM((2, FINE, NX), f32),
            pltpu.VMEM((2, 2, FINE, NY // 2), f32),
            pltpu.VMEM((2, 128, LANES), f32),
            pltpu.VMEM((NX, 256), bf16),
            pltpu.VMEM((NX, 256), bf16),
            pltpu.VMEM((256, NX), bf16),
            pltpu.VMEM((256, NX), bf16),
            pltpu.VMEM((2, 4, 2, 8, 2, OCT, 256), bf16),
            pltpu.VMEM((2, 64, 2, OCT, 256), bf16),
            pltpu.VMEM((2, 4, NY // 2, 256), bf16),
            pltpu.VMEM((2, 8 * OCT, NY // 2), bf16),
            pltpu.VMEM((4, 2, 8, LANES), f32),
            pltpu.VMEM((2, 2, 8 * OCT, 256), f32),
            pltpu.VMEM((OCTETS, 4, 2, 4, OCT, 2 * LANES), bf16),
            pltpu.VMEM((OCTETS, 4, 2, 4, OCT, 2 * LANES), bf16),
            pltpu.VMEM((OCTETS, 4, 4, OCT, LANES), f32),
            pltpu.SemaphoreType.DMA((6,)),
            pltpu.SemaphoreType.DMA((4,)),
            pltpu.SemaphoreType.DMA((3,)),
            pltpu.SemaphoreType.DMA((OCTETS,)),
            pltpu.SemaphoreType.DMA,
            pltpu.SemaphoreType.DMA,
        ],
        compiler_params=pltpu.CompilerParams(
            vmem_limit_bytes=60 << 20,
            **(dict(collective_id=0, has_side_effects=True) if comm else {}),
        ),
        name="render",
    )(spectrum, colour_table, map_index, jnp.asarray(fine_pair), jnp.asarray(fine_y), jnp.asarray(coarse_pair))


def solution(mesh):
    return jax.shard_map(
        render,
        mesh=mesh,
        in_specs=(P("depth", None, "plane", None), P(), P("depth")),
        out_specs=P(None, "plane", "depth"),
        check_vma=False,
    )
```

time: 51.9 us -> 49.5 us (0.954)
  Pallas kernels: 50.1 us -> 47.7 us
    pallas_call x1, Pallas kernels: 50.1 us -> 47.7 us  [render(): pl.pallas_call(functools.partial(kernel, comm=comm), out_shape=jax.ShapeD...]
where the time goes in v4:
time: 49.5 us; the launch traced here: 49.4 us
  Pallas kernels  47.7 us (96%)
  local copies, waits for them, and re-layouts  1.67 us (3%)
    pallas_call x1, Pallas kernels, render(): pl.pallas_call(functools.partial(kernel, comm=comm), out_shape=jax.ShapeD...  47.7 us
    unnamed x1, local copies, waits for them, and re-layouts  1.67 us

profile of v4, /device:TPU:1, one launch (start us, length us, event | category | flops | bytes accessed | tf_op | source)
XLA Modules:
  0.0 49.4 jit_solution(1709343352761169670)
XLA Ops:
  0.0 47.7 %render.1 = f32[4,128,128]{2,1,0:T(8,128)} custom-call(bf16[2,2,64,2048]{3,2,1,0:T(8,128)(2,1)} %spec_hbm.1, f32[4,4,16]{2,1,0:T(4,128)} %colour_hbm.1, s32[2]{0:T(128)} %map_hbm.1, f32[2,16,2048]{2,1,0:T(8,128)} %constant.6.clone.fine_hbm, f32[2,2,16,1024]{3,2,1,0:T(8,128)} %constant.7.clone.fine_y_hbm, f32[2,128,128]{2,1,0:T(8,128)} %constant.8.clone.coarse_hbm), custom_call_target="tpu_custom_call" | custom-call | tf_op jit(solution)/shard_map/render/pallas_call | solution.py:367
  47.8 1.7 %copy.8 = f32[4,128,128]{2,1,0:T(8,128)} copy(f32[4,128,128]{2,1,0:T(8,128)} %render.1) | data formatting | bytes 524288

commit v5 on v4

--- a/solution.py
+++ b/solution.py
@@ -36,7 +36,7 @@
 def kernel(
     spec_hbm, colour_hbm, map_hbm, fine_hbm, fine_y_hbm, coarse_hbm, out_ref,
     spec_ref, colour_ref, map_ref, fine_ref, fine_y_ref, coarse_ref,
-    turned_ref, swapped_ref, cos_ref, sin_ref, send1, recv1, ytab, lhs, ctab, dens, send2, recv2, send3,
+    turned_ref, swapped_ref, cos_ref, sin_ref, send1, recv1, ytab, lhs, ctab, dens, send2, recv2, send3, recv3,
     in_sem, send_sem, recv1_sem, recv2_sem, recv3_sem, tab_sem, *, comm
 ):
     if comm:
@@ -52,7 +52,7 @@
     fetches = [
         pltpu.make_async_copy(src, dst, in_sem.at[i])
         for i, (src, dst) in enumerate(
-            [(spec_hbm, spec_ref), (fine_hbm, fine_ref), (coarse_hbm, coarse_ref),
+            [(fine_hbm, fine_ref), (coarse_hbm, coarse_ref), (spec_hbm, spec_ref),
              (colour_hbm, colour_ref), (map_hbm, map_ref), (fine_y_hbm, fine_y_ref)]
         )
     ]
@@ -135,10 +135,10 @@
 
         lax.fori_loop(0, 8, send, 0)
 
+    fetches[0].wait()
     fetches[1].wait()
+    x_tables(0, 0)
     fetches[2].wait()
-    x_tables(0, 0)
-    fetches[0].wait()
 
     source = lax.broadcasted_iota(jnp.int32, (256, 256), 0)
     column = lax.broadcasted_iota(jnp.int32, (256, 256), 1)
@@ -289,16 +289,21 @@
                     total[q] = total[q] + clear * recv2[octet, x, half, q, :, cols].astype(jnp.float32)
                 clear = clear * (1.0 - recv2[octet, x, half, 3, :, cols].astype(jnp.float32))
             for q in range(4):
-                send3[octet, zl, q] = total[q] if q < 3 else clear
+                result = total[q] if q < 3 else clear
+                send3[octet, zl, q] = result.astype(jnp.bfloat16)
+
+                @pl.when(my_zl == zl)
+                def _(q=q, result=result):
+                    out_ref[q, rows, :] = result
+
             if comm:
                 @pl.when(my_zl != zl)
                 def _(zl=zl):
                     pltpu.make_async_remote_copy(
-                        src_ref=send3.at[octet, zl], dst_ref=out_ref.at[:, rows, :],
+                        src_ref=send3.at[octet, zl], dst_ref=recv3.at[octet, my_zl],
                         send_sem=send_sem.at[2], recv_sem=recv3_sem,
                         device_id=same_plane(my_x, zl), device_id_type=MESH,
                     ).start()
-        out_ref[:, rows, :] = send3[octet, my_zl]
 
     def slab(octet, carry):
         chunk, part = octet // 2, octet % 2
@@ -355,13 +360,20 @@
         waiting(recv1.at[:, pl.ds(0, 63)], 0, recv1_sem.at[0], next_z).wait_send()
         waiting(recv2.at[:, pl.ds(0, 3)], 1, recv2_sem.at[0], next_x).wait_send()
         last = waiting(send3.at[pl.ds(0, 3)], 2, recv3_sem, next_zl)
+        last.wait_recv()
+        for zl in range(4):
+            @pl.when(my_zl != zl)
+            def _(zl=zl):
+                for octet in range(OCTETS):
+                    rows = slice(zl * 32 + octet * OCT, zl * 32 + (octet + 1) * OCT)
+                    out_ref[:, rows, :] = recv3[octet, zl].astype(jnp.float32)
+
         last.wait_send()
-        last.wait_recv()
         table_copy().wait_send()
 
 
 def render(spectrum, colour_table, map_index, comm=True):
-    fine_pair, fine_y, coarse_pair = base_tables()
+    operands = [spectrum, colour_table, map_index, *map(jnp.asarray, base_tables())]
     vmem = pl.BlockSpec(memory_space=pltpu.VMEM)
     bf16, f32 = jnp.bfloat16, jnp.float32
     return pl.pallas_call(
@@ -388,7 +400,8 @@
             pltpu.VMEM((2, 2, 8 * OCT, 256), f32),
             pltpu.VMEM((OCTETS, 4, 2, 4, OCT, 2 * LANES), bf16),
             pltpu.VMEM((OCTETS, 4, 2, 4, OCT, 2 * LANES), bf16),
-            pltpu.VMEM((OCTETS, 4, 4, OCT, LANES), f32),
+            pltpu.VMEM((OCTETS, 4, 4, OCT, LANES), bf16),
+            pltpu.VMEM((OCTETS, 4, 4, OCT, LANES), bf16),
             pltpu.SemaphoreType.DMA((6,)),
             pltpu.SemaphoreType.DMA((4,)),
             pltpu.SemaphoreType.DMA((3,)),
@@ -397,11 +410,11 @@
             pltpu.SemaphoreType.DMA,
         ],
         compiler_params=pltpu.CompilerParams(
-            vmem_limit_bytes=60 << 20,
+            vmem_limit_bytes=40 << 20,
             **(dict(collective_id=0, has_side_effects=True) if comm else {}),
         ),
         name="render",
-    )(spectrum, colour_table, map_index, jnp.asarray(fine_pair), jnp.asarray(fine_y), jnp.asarray(coarse_pair))
+    )(*[pltpu.with_memory_space_constraint(operand, pltpu.HBM) for operand in operands])
 
 
 def solution(mesh):

time: 49.5 us -> 47.6 us (0.962)
  local copies, waits for them, and re-layouts: 1.67 us -> 0.71 us
  Pallas kernels: 47.7 us -> 46.9 us
    unnamed x1, local copies, waits for them, and re-layouts: 1.67 us -> 0.71 us
    pallas_call x1, Pallas kernels: 47.7 us -> 46.9 us  [render(): pl.pallas_call(functools.partial(kernel, comm=comm), out_shape=jax.ShapeD...]
where the time goes in v5:
time: 47.6 us
  Pallas kernels  46.9 us (99%)
  local copies, waits for them, and re-layouts  0.71 us (1%)
    pallas_call x1, Pallas kernels, render(): pl.pallas_call(functools.partial(kernel, comm=comm), out_shape=jax.ShapeD...  46.9 us

profile of v5, /device:TPU:1, one launch (start us, length us, event | category | flops | bytes accessed | tf_op | source)
XLA Modules:
  0.0 47.6 jit_solution(2695989349128298268)
XLA Ops:
  0.0 46.9 %render.1 = f32[4,128,128]{2,1,0:T(8,128)S(1)} custom-call(bf16[2,2,64,2048]{3,2,1,0:T(8,128)(2,1)} %spec_hbm.1, f32[4,4,16]{2,1,0:T(4,128)} %colour_hbm.1, s32[2]{0:T(128)} %map_hbm.1, f32[2,16,2048]{2,1,0:T(8,128)} %constant.6.clone.fine_hbm, f32[2,2,16,1024]{3,2,1,0:T(8,128)} %constant.7.clone.fine_y_hbm, f32[2,128,128]{2,1,0:T(8,128)} %constant.8.clone.coarse_hbm), custom_call_target="tpu_custom_call" | custom-call | tf_op jit(solution)/shard_map/render/pallas_call | solution.py:379
  46.9 0.7 %copy.8 = f32[4,128,128]{2,1,0:T(8,128)} copy(f32[4,128,128]{2,1,0:T(8,128)S(1)} %render.1) | data formatting | bytes 524288

commit v6 on v5

--- a/solution.py
+++ b/solution.py
@@ -36,8 +36,8 @@
 def kernel(
     spec_hbm, colour_hbm, map_hbm, fine_hbm, fine_y_hbm, coarse_hbm, out_ref,
     spec_ref, colour_ref, map_ref, fine_ref, fine_y_ref, coarse_ref,
-    turned_ref, swapped_ref, cos_ref, sin_ref, send1, recv1, ytab, lhs, ctab, dens, send2, recv2, send3, recv3,
-    in_sem, send_sem, recv1_sem, recv2_sem, recv3_sem, tab_sem, *, comm
+    turned_ref, swapped_ref, cos_ref, sin_ref, send1, recv1, ytab, lhs, ctab, dens, send2, recv2, send3, recv3, direct,
+    in_sem, send_sem, recv1_sem, recv2_sem, recv3_sem, direct_sem, tab_sem, *, comm
 ):
     if comm:
         depth_id = lax.axis_index("depth")
@@ -75,12 +75,12 @@
 
         def greet_depth(i, carry):
             pl.semaphore_signal(
-                barrier, inc=1, device_id=same_plane((my_x + i) % 4, my_zl), device_id_type=MESH
+                barrier, inc=1, device_id=same_plane((my_x + 1 + i // 4) % 4, i % 4), device_id_type=MESH
             )
             return carry
 
         lax.fori_loop(1, 64, greet_gather, 0)
-        lax.fori_loop(1, 4, greet_depth, 0)
+        lax.fori_loop(0, 12, greet_depth, 0)
 
     x_scale = 1.0 / math.sqrt(NX)
     y_scale = math.sqrt(2.0 / NY)
@@ -167,7 +167,7 @@
         ctab[my_zl, z] = jnp.concatenate([values, slopes], axis=0)
 
     if comm:
-        pl.semaphore_wait(barrier, 66)
+        pl.semaphore_wait(barrier, 75)
     send_x(0, 0)
     if comm:
         for k in range(1, 4):
@@ -268,13 +268,53 @@
                 result = colour[i, c][q] if q < 3 else 1.0 - clear[i, c]
                 send2[octet, xs[i], half, q, :, c * LANES : (c + 1) * LANES] = result.astype(jnp.bfloat16)
 
-    def send_x_part(octet, x, half):
+    def columns_of(c):
+        return slice(c * LANES, (c + 1) * LANES)
+
+    def send_part(octet, x, half, own=False):
+        if not comm:
+            return
+
+        if not own:
+            @pl.when(octet < OCTETS - 1)
+            def _():
+                pltpu.make_async_remote_copy(
+                    src_ref=send2.at[octet, x, half], dst_ref=recv2.at[octet, my_x, half],
+                    send_sem=send_sem.at[1], recv_sem=recv2_sem.at[octet],
+                    device_id=same_plane(x, my_zl), device_id_type=MESH,
+                ).start()
+
+        @pl.when(octet == OCTETS - 1)
+        def _():
+            for c in range(2):
+                zl = 2 * half + c
+                copy = pltpu.make_async_remote_copy(
+                    src_ref=send2.at[OCTETS - 1, x, half, :, :, columns_of(c)],
+                    dst_ref=direct.at[my_x * 4 + my_zl], send_sem=send_sem.at[4], recv_sem=direct_sem,
+                    device_id=same_plane(x, zl), device_id_type=MESH,
+                )
+                if own:
+                    pl.when(zl != my_zl)(copy.start)
+                else:
+                    copy.start()
+
+    def over(parts):
+        total = [parts(0, q).astype(jnp.float32) for q in range(3)]
+        clear = 1.0 - parts(0, 3).astype(jnp.float32)
+        for x in range(1, 4):
+            for q in range(3):
+                total[q] = total[q] + clear * parts(x, q).astype(jnp.float32)
+            clear = clear * (1.0 - parts(x, 3).astype(jnp.float32))
+        return [*total, clear]
+
+    def combine_last():
         if comm:
-            pltpu.make_async_remote_copy(
-                src_ref=send2.at[octet, x, half], dst_ref=recv2.at[octet, my_x, half],
-                send_sem=send_sem.at[1], recv_sem=recv2_sem.at[octet],
-                device_id=same_plane(x, my_zl), device_id_type=MESH,
-            ).start()
+            waiting(direct.at[pl.ds(0, 15)], 4, direct_sem, next_x).wait_recv()
+        for zl in range(4):
+            rows = slice(zl * 32 + 3 * OCT, zl * 32 + 4 * OCT)
+            result = over(lambda x, q, zl=zl: direct[x * 4 + zl, q])
+            for q in range(4):
+                out_ref[q, rows, :] = result[q]
 
     def combine(octet):
         if comm:
@@ -282,14 +322,9 @@
         rows = pl.ds(pl.multiple_of(my_zl * 32 + octet * OCT, OCT), OCT)
         for zl in range(4):
             half, cols = zl // 2, slice((zl % 2) * LANES, (zl % 2 + 1) * LANES)
-            total = [recv2[octet, 0, half, q, :, cols].astype(jnp.float32) for q in range(3)]
-            clear = 1.0 - recv2[octet, 0, half, 3, :, cols].astype(jnp.float32)
-            for x in range(1, 4):
-                for q in range(3):
-                    total[q] = total[q] + clear * recv2[octet, x, half, q, :, cols].astype(jnp.float32)
-                clear = clear * (1.0 - recv2[octet, x, half, 3, :, cols].astype(jnp.float32))
+            results = over(lambda x, q, half=half, cols=cols: recv2[octet, x, half, q, :, cols])
             for q in range(4):
-                result = total[q] if q < 3 else clear
+                result = results[q]
                 send3[octet, zl, q] = result.astype(jnp.bfloat16)
 
                 @pl.when(my_zl == zl)
@@ -332,39 +367,52 @@
         others = [(my_x + 1) % 4, (my_x + 3) % 4]
         across = (my_x + 2) % 4
         for piece in range(8):
-            transform_y(theirs, 0, piece)
-        shade(octet, others, 0, 0, (theirs + 1, 1))
+            transform_y(theirs + 1 - my_zl // 2, 0, piece)
+        far, near = 1 - my_zl // 2, my_zl // 2
+        shade(octet, others, far, 0, (theirs + near, 1))
         for x in others:
-            send_x_part(octet, x, 0)
-        shade(octet, others, 1, 1, (ours, 0))
+            send_part(octet, x, far)
+        shade(octet, others, near, 1, (ours + far, 0))
         for x in others:
-            send_x_part(octet, x, 1)
-        shade(octet, [across], 0, 0, (ours + 1, 1))
-        send_x_part(octet, across, 0)
-        shade(octet, [across], 1, 1, None)
-        send_x_part(octet, across, 1)
-        shade(octet, [my_x], 0, 0, None)
-        shade(octet, [my_x], 1, 1, None)
-        recv2[octet, my_x] = send2[octet, my_x]
+            send_part(octet, x, near)
+        shade(octet, [across], far, 0, (ours + near, 1))
+        send_part(octet, across, far)
+        shade(octet, [across], near, 1, None)
+        send_part(octet, across, near)
 
         @pl.when(octet > 0)
         def _():
             combine(octet - 1)
 
+        shade(octet, [my_x], far, 0, None)
+        send_part(octet, my_x, far, own=True)
+        shade(octet, [my_x], near, 1, None)
+        send_part(octet, my_x, near, own=True)
+
+        @pl.when(octet < OCTETS - 1)
+        def _():
+            recv2[octet, my_x] = send2[octet, my_x]
+
         return carry
 
     lax.fori_loop(0, OCTETS, slab, 0)
-    combine(OCTETS - 1)
+    for c in range(2):
+        @pl.when(my_zl % 2 == c)
+        def _(c=c):
+            direct[depth_id] = send2[OCTETS - 1, my_x, my_zl // 2, :, :, columns_of(c)]
+
+    combine_last()
 
     if comm:
         waiting(recv1.at[:, pl.ds(0, 63)], 0, recv1_sem.at[0], next_z).wait_send()
-        waiting(recv2.at[:, pl.ds(0, 3)], 1, recv2_sem.at[0], next_x).wait_send()
-        last = waiting(send3.at[pl.ds(0, 3)], 2, recv3_sem, next_zl)
+        waiting(recv2.at[pl.ds(0, 3), pl.ds(0, 3)], 1, recv2_sem.at[0], next_x).wait_send()
+        waiting(direct.at[pl.ds(0, 15)], 4, direct_sem, next_x).wait_send()
+        last = waiting(send3.at[:, pl.ds(0, 3)], 2, recv3_sem, next_zl)
         last.wait_recv()
         for zl in range(4):
             @pl.when(my_zl != zl)
             def _(zl=zl):
-                for octet in range(OCTETS):
+                for octet in range(OCTETS - 1):
                     rows = slice(zl * 32 + octet * OCT, zl * 32 + (octet + 1) * OCT)
                     out_ref[:, rows, :] = recv3[octet, zl].astype(jnp.float32)
 
@@ -399,13 +447,15 @@
             pltpu.VMEM((4, 2, 8, LANES), f32),
             pltpu.VMEM((2, 2, 8 * OCT, 256), f32),
             pltpu.VMEM((OCTETS, 4, 2, 4, OCT, 2 * LANES), bf16),
-            pltpu.VMEM((OCTETS, 4, 2, 4, OCT, 2 * LANES), bf16),
-            pltpu.VMEM((OCTETS, 4, 4, OCT, LANES), bf16),
-            pltpu.VMEM((OCTETS, 4, 4, OCT, LANES), bf16),
+            pltpu.VMEM((OCTETS - 1, 4, 2, 4, OCT, 2 * LANES), bf16),
+            pltpu.VMEM((OCTETS - 1, 4, 4, OCT, LANES), bf16),
+            pltpu.VMEM((OCTETS - 1, 4, 4, OCT, LANES), bf16),
+            pltpu.VMEM((16, 4, OCT, LANES), bf16),
             pltpu.SemaphoreType.DMA((6,)),
-            pltpu.SemaphoreType.DMA((4,)),
+            pltpu.SemaphoreType.DMA((5,)),
             pltpu.SemaphoreType.DMA((3,)),
-            pltpu.SemaphoreType.DMA((OCTETS,)),
+            pltpu.SemaphoreType.DMA((OCTETS - 1,)),
+            pltpu.SemaphoreType.DMA,
             pltpu.SemaphoreType.DMA,
             pltpu.SemaphoreType.DMA,
         ],

time: 47.6 us -> 46.5 us (0.977)
  Pallas kernels: 46.9 us -> 45.7 us
    pallas_call x1, Pallas kernels: 46.9 us -> 45.7 us  [render(): pl.pallas_call(functools.partial(kernel, comm=comm), out_shape=jax.ShapeD...]
where the time goes in v6:
time: 46.5 us
  Pallas kernels  45.7 us (98%)
  local copies, waits for them, and re-layouts  0.71 us (2%)
    pallas_call x1, Pallas kernels, render(): pl.pallas_call(functools.partial(kernel, comm=comm), out_shape=jax.ShapeD...  45.7 us

profile of v6, /device:TPU:1, one launch (start us, length us, event | category | flops | bytes accessed | tf_op | source)
XLA Modules:
  0.0 46.5 jit_solution(18124763452497894543)
XLA Ops:
  0.0 45.7 %render.1 = f32[4,128,128]{2,1,0:T(8,128)S(1)} custom-call(bf16[2,2,64,2048]{3,2,1,0:T(8,128)(2,1)} %spec_hbm.1, f32[4,4,16]{2,1,0:T(4,128)} %colour_hbm.1, s32[2]{0:T(128)} %map_hbm.1, f32[2,16,2048]{2,1,0:T(8,128)} %constant.6.clone.fine_hbm, f32[2,2,16,1024]{3,2,1,0:T(8,128)} %constant.7.clone.fine_y_hbm, f32[2,128,128]{2,1,0:T(8,128)} %constant.8.clone.coarse_hbm), custom_call_target="tpu_custom_call" | custom-call | tf_op jit(solution)/shard_map/render/pallas_call | solution.py:427
  45.8 0.7 %copy.8 = f32[4,128,128]{2,1,0:T(8,128)} copy(f32[4,128,128]{2,1,0:T(8,128)S(1)} %render.1) | data formatting | bytes 524288

commit v7 on v6

--- a/solution.py
+++ b/solution.py
@@ -110,14 +110,21 @@
         rows += jnp.dot(sin_ref[...], swapped_ref[...], preferred_element_type=jnp.float32)
         send1[chunk, k] = rows.reshape(2, 8, 2, OCT, 256).astype(jnp.bfloat16)
 
-    def send_x(k, part):
+    def x_side(side):
+        half = slice(128 * side, 128 * (side + 1))
+        rows = jnp.dot(cos_ref[half, :], turned_ref[...], preferred_element_type=jnp.float32)
+        rows += jnp.dot(sin_ref[half, :], swapped_ref[...], preferred_element_type=jnp.float32)
+        send1[0, 0, side] = rows.reshape(8, 2, OCT, 256).astype(jnp.bfloat16)
+
+    def send_x(k, part, sides=(0, 1)):
         zs = pair_z(k)
         if not comm:
             return
 
         def send(i, c):
             j = (my_j + i) % 8
-            for side, z in enumerate(zs):
+            for side in sides:
+                z = zs[side]
                 if part == 0:
                     src, dst = send1.at[0, k, side, j], recv1.at[0, my_zl * 16 + plane_id]
                 else:
@@ -151,10 +158,18 @@
     ).astype(jnp.bfloat16)
     tn = (((0,), (0,)), ((), ()))
     spec = spec_ref[...].reshape(256, NX)
-    turned_ref[...] = lax.dot_general(spec, straight, tn, preferred_element_type=jnp.float32).astype(jnp.bfloat16)
-    swapped_ref[...] = lax.dot_general(spec, crossed, tn, preferred_element_type=jnp.float32).astype(jnp.bfloat16)
-
-    x_rows(0, 0)
+    both = lax.dot_general(
+        spec, jnp.concatenate([straight, crossed], axis=1), tn, preferred_element_type=jnp.float32
+    ).astype(jnp.bfloat16)
+    turned_ref[...] = both[:, :256]
+    swapped_ref[...] = both[:, 256:]
+
+    x_side(0)
+    if comm:
+        pl.semaphore_wait(barrier, 75)
+    send_x(0, 0, sides=(0,))
+    x_side(1)
+    send_x(0, 0, sides=(1,))
     fetches[3].wait()
     fetches[4].wait()
 
@@ -166,9 +181,6 @@
         slopes = pltpu.roll(values, LANES - 1, 1) - values
         ctab[my_zl, z] = jnp.concatenate([values, slopes], axis=0)
 
-    if comm:
-        pl.semaphore_wait(barrier, 75)
-    send_x(0, 0)
     if comm:
         for k in range(1, 4):
             pltpu.make_async_remote_copy(
@@ -401,14 +413,8 @@
         def _(c=c):
             direct[depth_id] = send2[OCTETS - 1, my_x, my_zl // 2, :, :, columns_of(c)]
 
-    combine_last()
-
-    if comm:
-        waiting(recv1.at[:, pl.ds(0, 63)], 0, recv1_sem.at[0], next_z).wait_send()
-        waiting(recv2.at[pl.ds(0, 3), pl.ds(0, 3)], 1, recv2_sem.at[0], next_x).wait_send()
-        waiting(direct.at[pl.ds(0, 15)], 4, direct_sem, next_x).wait_send()
-        last = waiting(send3.at[:, pl.ds(0, 3)], 2, recv3_sem, next_zl)
-        last.wait_recv()
+    if comm:
+        waiting(send3.at[:, pl.ds(0, 3)], 2, recv3_sem, next_zl).wait_recv()
         for zl in range(4):
             @pl.when(my_zl != zl)
             def _(zl=zl):
@@ -416,7 +422,13 @@
                     rows = slice(zl * 32 + octet * OCT, zl * 32 + (octet + 1) * OCT)
                     out_ref[:, rows, :] = recv3[octet, zl].astype(jnp.float32)
 
-        last.wait_send()
+    combine_last()
+
+    if comm:
+        waiting(recv1.at[:, pl.ds(0, 63)], 0, recv1_sem.at[0], next_z).wait_send()
+        waiting(recv2.at[pl.ds(0, 3), pl.ds(0, 3)], 1, recv2_sem.at[0], next_x).wait_send()
+        waiting(direct.at[pl.ds(0, 15)], 4, direct_sem, next_x).wait_send()
+        waiting(send3.at[:, pl.ds(0, 3)], 2, recv3_sem, next_zl).wait_send()
         table_copy().wait_send()
 
 

time: 46.5 us -> 46.1 us (level)
  no operation moved by 1% of the time
where the time goes in v7:
time: 46.1 us
  Pallas kernels  45.4 us (98%)
  local copies, waits for them, and re-layouts  0.71 us (2%)
    pallas_call x1, Pallas kernels, render(): pl.pallas_call(functools.partial(kernel, comm=comm), out_shape=jax.ShapeD...  45.4 us

profile of v7, /device:TPU:1, one launch (start us, length us, event | category | flops | bytes accessed | tf_op | source)
XLA Modules:
  0.0 46.1 jit_solution(3429268159035973491)
XLA Ops:
  0.0 45.4 %render.1 = f32[4,128,128]{2,1,0:T(8,128)S(1)} custom-call(bf16[2,2,64,2048]{3,2,1,0:T(8,128)(2,1)} %spec_hbm.1, f32[4,4,16]{2,1,0:T(4,128)} %colour_hbm.1, s32[2]{0:T(128)} %map_hbm.1, f32[2,16,2048]{2,1,0:T(8,128)} %constant.6.clone.fine_hbm, f32[2,2,16,1024]{3,2,1,0:T(8,128)} %constant.7.clone.fine_y_hbm, f32[2,128,128]{2,1,0:T(8,128)} %constant.8.clone.coarse_hbm), custom_call_target="tpu_custom_call" | custom-call | tf_op jit(solution)/shard_map/render/pallas_call | solution.py:439
  45.4 0.7 %copy.8 = f32[4,128,128]{2,1,0:T(8,128)} copy(f32[4,128,128]{2,1,0:T(8,128)S(1)} %render.1) | data formatting | bytes 524288

commit v8 on v7

--- a/solution.py
+++ b/solution.py
@@ -33,6 +33,14 @@
     return fine_pair, fine_y, coarse_pair
 
 
+def quotient(a, b):
+    return a // b if isinstance(a, int) else lax.div(a, jnp.int32(b))
+
+
+def remainder(a, b):
+    return a % b if isinstance(a, int) else lax.rem(a, jnp.int32(b))
+
+
 def kernel(
     spec_hbm, colour_hbm, map_hbm, fine_hbm, fine_y_hbm, coarse_hbm, out_ref,
     spec_ref, colour_ref, map_ref, fine_ref, fine_y_ref, coarse_ref,
@@ -60,7 +68,7 @@
         fetch.start()
 
     def same_x(z, j):
-        return {"depth": my_x * 4 + z % 4, "plane": (z // 4) * 8 + j}
+        return {"depth": my_x * 4 + remainder(z, 4), "plane": quotient(z, 4) * 8 + j}
 
     def same_plane(x, zl):
         return {"depth": x * 4 + zl, "plane": plane_id}
@@ -69,13 +77,13 @@
         barrier = pltpu.get_barrier_semaphore()
 
         def greet_gather(i, carry):
-            z, j = (my_z + i // 8) % 8, (my_j + i % 8) % 8
+            z, j = remainder(my_z + quotient(i, 8), 8), remainder(my_j + remainder(i, 8), 8)
             pl.semaphore_signal(barrier, inc=1, device_id=same_x(z, j), device_id_type=MESH)
             return carry
 
         def greet_depth(i, carry):
             pl.semaphore_signal(
-                barrier, inc=1, device_id=same_plane((my_x + 1 + i // 4) % 4, i % 4), device_id_type=MESH
+                barrier, inc=1, device_id=same_plane(remainder(my_x + 1 + quotient(i, 4), 4), remainder(i, 4)), device_id_type=MESH
             )
             return carry
 
@@ -91,11 +99,11 @@
         return jnp.broadcast_to(bc, (FINE, LANES)), jnp.broadcast_to(bs, (FINE, LANES))
 
     def pair_z(k):
-        return (my_z + 4 - k) % 8, (my_z + 4 + k + 4 * ((4 - k) // 4)) % 8
+        return remainder(my_z + 4 - k, 8), remainder(my_z + 4 + k + 4 * quotient(4 - k, 4), 8)
 
     def x_tables(chunk, k):
         for i, z in enumerate(pair_z(k)):
-            first = (z // 4) * 64 + 2 * (z % 4) + chunk
+            first = quotient(z, 4) * 64 + 2 * remainder(z, 4) + chunk
             for j in range(8):
                 bc, bs = coarse_row(first + 8 * j, x_scale)
                 rows = slice((8 * i + j) * FINE, (8 * i + j + 1) * FINE)
@@ -122,7 +130,7 @@
             return
 
         def send(i, c):
-            j = (my_j + i) % 8
+            j = remainder(my_j + i, 8)
             for side in sides:
                 z = zs[side]
                 if part == 0:

time: 46.1 us -> 46.1 us (level)
  no operation moved by 1% of the time
where the time goes in v8:
time: 46.1 us; the launch traced here: 46 us
  Pallas kernels  45.3 us (98%)
  local copies, waits for them, and re-layouts  0.71 us (2%)
    pallas_call x1, Pallas kernels, render(): pl.pallas_call(functools.partial(kernel, comm=comm), out_shape=jax.ShapeD...  45.3 us

profile of v8, /device:TPU:1, one launch (start us, length us, event | category | flops | bytes accessed | tf_op | source)
XLA Modules:
  0.0 46.0 jit_solution(9441999497951228554)
XLA Ops:
  0.0 45.3 %render.1 = f32[4,128,128]{2,1,0:T(8,128)S(1)} custom-call(bf16[2,2,64,2048]{3,2,1,0:T(8,128)(2,1)} %spec_hbm.1, f32[4,4,16]{2,1,0:T(4,128)} %colour_hbm.1, s32[2]{0:T(128)} %map_hbm.1, f32[2,16,2048]{2,1,0:T(8,128)} %constant.6.clone.fine_hbm, f32[2,2,16,1024]{3,2,1,0:T(8,128)} %constant.7.clone.fine_y_hbm, f32[2,128,128]{2,1,0:T(8,128)} %constant.8.clone.coarse_hbm), custom_call_target="tpu_custom_call" | custom-call | tf_op jit(solution)/shard_map/render/pallas_call | solution.py:447
  45.3 0.7 %copy.8 = f32[4,128,128]{2,1,0:T(8,128)} copy(f32[4,128,128]{2,1,0:T(8,128)S(1)} %render.1) | data formatting | bytes 524288

commit v9 on v7

--- a/solution.py
+++ b/solution.py
@@ -246,10 +246,8 @@
 
     low = lax.broadcasted_iota(jnp.int32, (OCT, LANES), 1) < 64
 
-    def transform_y(block, slot, piece):
-        parity, depth = piece // 4, slice((piece % 4) * 256, (piece % 4 + 1) * 256)
-        part = jnp.dot(lhs[parity, :, depth], ytab[parity, block, depth, :], preferred_element_type=jnp.float32)
-        dens[slot, parity] = part if piece % 4 == 0 else dens[slot, parity] + part
+    def transform_y(block, slot, parity):
+        dens[slot, parity] = jnp.dot(lhs[parity], ytab[parity, block], preferred_element_type=jnp.float32)
 
     def shade(octet, xs, half, slot, following):
         tiles = [(i, c) for i in range(len(xs)) for c in range(2)]
@@ -257,8 +255,8 @@
         colour = {t: [jnp.zeros((OCT, LANES), jnp.float32) for _ in range(3)] for t in tiles}
         clear = {t: jnp.ones((OCT, LANES), jnp.float32) for t in tiles}
         for z in range(8):
-            if following is not None:
-                transform_y(*following, z)
+            if following is not None and z % 4 == 0:
+                transform_y(*following, z // 4)
             maps = [jnp.broadcast_to(ctab[z // 2, z % 2, q : q + 1, :], (OCT, LANES)) for q in range(8)]
             for t in tiles:
                 i, c = t
@@ -378,8 +376,8 @@
         ours = 2 * (my_x % 2)
         others = [(my_x + 1) % 4, (my_x + 3) % 4]
         across = (my_x + 2) % 4
-        for piece in range(8):
-            transform_y(theirs + 1 - my_zl // 2, 0, piece)
+        for parity in range(2):
+            transform_y(theirs + 1 - my_zl // 2, 0, parity)
         far, near = 1 - my_zl // 2, my_zl // 2
         shade(octet, others, far, 0, (theirs + near, 1))
         for x in others:

time: 46.1 us -> 46.1 us (level)
  no operation moved by 1% of the time
where the time goes in v9:
time: 46.1 us
  Pallas kernels  45.4 us (98%)
  local copies, waits for them, and re-layouts  0.71 us (2%)
    pallas_call x1, Pallas kernels, render(): pl.pallas_call(functools.partial(kernel, comm=comm), out_shape=jax.ShapeD...  45.4 us

profile of v9, /device:TPU:1, one launch (start us, length us, event | category | flops | bytes accessed | tf_op | source)
XLA Modules:
  0.0 46.1 jit_solution(3429268159035973491)
XLA Ops:
  0.0 45.4 %render.1 = f32[4,128,128]{2,1,0:T(8,128)S(1)} custom-call(bf16[2,2,64,2048]{3,2,1,0:T(8,128)(2,1)} %spec_hbm.1, f32[4,4,16]{2,1,0:T(4,128)} %colour_hbm.1, s32[2]{0:T(128)} %map_hbm.1, f32[2,16,2048]{2,1,0:T(8,128)} %constant.6.clone.fine_hbm, f32[2,2,16,1024]{3,2,1,0:T(8,128)} %constant.7.clone.fine_y_hbm, f32[2,128,128]{2,1,0:T(8,128)} %constant.8.clone.coarse_hbm), custom_call_target="tpu_custom_call" | custom-call | tf_op jit(solution)/shard_map/render/pallas_call | solution.py:437
  45.4 0.7 %copy.8 = f32[4,128,128]{2,1,0:T(8,128)} copy(f32[4,128,128]{2,1,0:T(8,128)S(1)} %render.1) | data formatting | bytes 524288
